TPU v7x, 32 devices: a whole 2x2x4 slice. The times are simulated.
32 devices in a mesh: node: 4 (over y, core), cores: 8 (over z, x).
Axes of the slice: x: 2, y: 2, z: 4, core: 2. Of those that a mesh axis runs over, the one named last changes fastest.
Arguments:
- adjoint: bfloat16 [256, 2, 128, 128], P(('node', 'cores')), may hold values from -6 to 6
- saved: bfloat16 [2, 4, 256, 2, 128, 128], P(None, None, ('node', 'cores')), may hold values from -0.046875 to 0.046875
- propagators: bfloat16 [2, 4, 2, 128, 128], replicated, may hold values from -3 to 3, as said below
- coupling: bfloat16 [128, 128], replicated, may hold values from -0.5 to 0.5
- higher: int32 [256, 4], replicated, may hold values from 0 to 255, as said below
- lower: int32 [256, 4], replicated, may hold values from 0 to 255, as said below
- ladder: int32 [2, 256, 4], P(None, ('node', 'cores')), may hold values from 0 to 3
- rates: float32 [2, 4], replicated, may hold values from 0.1 to 0.4
- decay: float32 [256], P(('node', 'cores')), may hold values from 0.4 to 1
Outputs:
- adjoint_out: bfloat16 [256, 2, 128, 128], P(('node', 'cores'))
- gradient: float32 [128, 8, 2, 128], P(('node', 'cores'))
Inputs may be any that keep to these rules, and one draw needn't show every extreme that they name: Density j lives on owner j // 8. Taken in the order of density then mode, the 32 higher-tier partners of one owner's densities lie on distinct owners when 8 * 4 <= 32, and else exactly 1 of them lie on each owner. The same holds for the lower-tier partners. `propagators`: A propagator substep is close to unitary.
All inputs are finite; a program needn't handle non-finite values.
Results may differ from a plain program's by a relative error of at most 0.024.
Values may be sent and summed in bfloat16 or wider, within the bound.
A program may use at most 128 MiB of HBM per device.

v0:
```python
import functools

import jax
import jax.numpy as jnp
from jax import lax
from jax.experimental import pallas as pl
from jax.experimental.pallas import tpu as pltpu
from jax.sharding import PartitionSpec as P

MESH = pl.DeviceIdType.MESH
F32 = jnp.float32
BF16 = jnp.bfloat16


def dot(a, b):
    return jnp.dot(a, b, preferred_element_type=F32)


def kernel(
    dims,
    picks,
    higher,
    lower,
    ladder,
    rates,
    decay,
    adjoint,
    saved_in,
    propagators,
    coupling,
    out,
    grad,
    right_u,
    left_u,
    hist,
    stage,
    inbox,
    terms,
    term_stage,
    term_inbox,
    saved,
    saved_t,
    *rest,
):
    nodes, depth, width, count, modes, steps, subs, dim, halves = dims
    hops = depth - 1
    chain = rest[: 2 * steps * hops]
    chain_send, chain_recv, plane_send, plane_recv, term_send, term_recv, local, credit = rest[
        2 * steps * hops :
    ]
    cores = depth * width
    owners = nodes * cores
    lanes = nodes * width
    rows = dim // owners
    batch = subs // halves
    node = lax.axis_index("node")
    spot = lax.axis_index("cores")
    level = spot // width
    column = spot % width
    lane = node * width + column

    def lane_of(offset):
        pair = 2 if nodes % 2 == 0 else 1
        far = lax.rem(node // pair + offset // (pair * width), nodes // pair)
        near = lax.rem(node + offset // width, pair)
        return (far * pair + near) * width + lax.rem(column + offset, width)

    def lane_id(other):
        return (other // width, level * width + other % width)

    def level_id(other):
        return (node, other * width + column)

    def owner_of(a_lane, a_level):
        return (a_lane // width) * cores + a_level * width + a_lane % width

    barrier = pltpu.get_barrier_semaphore()

    own = node * cores + spot

    def owner_id(offset):
        other = lax.rem(own + offset, owners)
        return (other // cores, lax.rem(other, cores))

    def greet(offset, carry):
        pl.semaphore_signal(barrier, inc=1, device_id=owner_id(offset), device_id_type=MESH)
        return carry

    lax.fori_loop(1, owners, greet, 0)
    fetch = pltpu.make_async_copy(saved_in, saved, local.at[0])
    fetch.start()

    def chain_block(step, way, hop):
        return chain[(step * 2 + way) * hops + hop - 1]

    def chain_copy(step, way, hop, source):
        peer = level + 1 if way == 0 else level - 1
        return pltpu.make_async_remote_copy(
            src_ref=source,
            dst_ref=chain_block(step, way, hop),
            send_sem=chain_send.at[step, way, hop - 1],
            recv_sem=chain_recv.at[step, way, hop - 1],
            device_id=level_id(peer),
            device_id_type=MESH,
        )

    def from_level(way, hop):
        return level - hop if way == 0 else level + hop

    def arrives(way, hop):
        return level >= hop if way == 0 else level + hop < depth

    def goes_on(way, hop):
        if way == 0:
            return jnp.logical_and(level >= hop - 1, level < depth - 1)
        return jnp.logical_and(level + hop - 1 < depth, level > 0)

    def plane_copy(offset, a_level):
        return pltpu.make_async_remote_copy(
            src_ref=stage.at[offset - 1, a_level],
            dst_ref=inbox.at[owner_of(lane, a_level)],
            send_sem=plane_send.at[offset - 1, a_level],
            recv_sem=plane_recv.at[owner_of(lane, a_level)],
            device_id=lane_id(lane_of(offset)),
            device_id_type=MESH,
        )

    def serve(block, a_level):
        fill_stage(block, a_level)
        send_stage(a_level)

    def fill_stage(block, a_level):
        source = owner_of(lane, a_level)

        def pick(offset, way):
            target = owner_of(lane_of(offset), level)
            return picks[way * owners + source, target]

        for way in range(2):
            inbox[source, way] = block[pick(0, way)]

        def fill(offset, carry):
            for way in range(2):
                stage[offset - 1, a_level, way] = block[pick(offset, way)]
            return carry

        lax.fori_loop(1, lanes, fill, 0)

    def send_stage(a_level):
        def send(offset, carry):
            plane_copy(offset, a_level).start()
            return carry

        lax.fori_loop(1, lanes, send, 0)

    def prepare():
        def one(at, carry):
            step, sub = at // subs, at % subs
            u_re = propagators[step, sub, 0]
            u_im = propagators[step, sub, 1]
            right_u[at, :dim, :dim] = u_re
            right_u[at, :dim, dim:] = u_im
            right_u[at, dim:, :dim] = -u_im
            right_u[at, dim:, dim:] = u_re
            t_re = u_re.T
            t_im = u_im.T
            left_u[at, :dim, :dim] = t_re
            left_u[at, :dim, dim:] = t_im
            left_u[at, dim:, :dim] = -t_im
            left_u[at, dim:, dim:] = t_re
            return carry

        lax.fori_loop(0, steps * subs, one, 0)

    def turn(sub):
        for j in range(count):
            kept = saved[steps - 1, sub, j].reshape(2 * dim, dim)
            saved_t[sub, :, 2 * dim * j : 2 * dim * (j + 1)] = kept.T

    def project(step, sub):
        total = jnp.zeros((dim, 2 * dim), F32)
        for j in range(count):
            lam_re = hist[step, sub + 1, j, 0]
            lam_im = hist[step, sub + 1, j, 1]
            both = jnp.concatenate(
                [
                    jnp.concatenate([lam_re, lam_im], axis=1),
                    jnp.concatenate([lam_im, -lam_re], axis=1),
                ],
                axis=0,
            )
            if step == steps - 1:
                kept_t = saved_t[sub, :, 2 * dim * j : 2 * dim * (j + 1)]
                total = total + dot(kept_t, both)
            else:
                kept = saved[step, sub, j].reshape(2 * dim, dim)
                total = total + lax.dot_general(
                    kept, both, (((0,), (0,)), ((), ())), preferred_element_type=F32
                )
        terms[sub % batch] = total
        if sub % batch == batch - 1:
            spread(step * halves + sub // batch)

    def spread(group):
        for target in range(owners):
            term_stage[group, target] = jnp.concatenate(
                [terms[i, target * rows : (target + 1) * rows] for i in range(batch)], axis=0
            ).astype(BF16)

        def send(offset, carry):
            pltpu.make_async_remote_copy(
                src_ref=term_stage.at[group, lax.rem(own + offset, owners)],
                dst_ref=term_inbox.at[group, offset - 1],
                send_sem=term_send.at[group],
                recv_sem=term_recv.at[group],
                device_id=owner_id(offset),
                device_id_type=MESH,
            ).start()
            return carry

        lax.fori_loop(1, owners, send, 0)

    def finish(group):
        everything = term_inbox.at[group]
        pltpu.make_async_copy(everything, everything, term_recv.at[group]).wait()
        total = term_stage[group, own].astype(F32)
        for offset in range(1, owners):
            total = total + term_inbox[group, offset - 1].astype(F32)
        for i in range(batch):
            for row in range(rows):
                for part in range(2):
                    grad[row, group * batch + i, part : part + 1, :] = total[
                        i * rows + row : i * rows + row + 1, part * dim : (part + 1) * dim
                    ]
        pltpu.make_async_copy(everything, everything, term_send.at[group]).wait()

    def couple(step, state):
        operator = coupling[...]

        def one(j, carry):
            plus, minus = [], []
            for part in range(2):
                sums = []
                for way in range(2):
                    total = jnp.zeros((dim, dim), F32)
                    for mode in range(modes):
                        weight = ladder[way, mode, j].astype(F32) * rates[way, mode]
                        place = lax.div((higher, lower)[way][mode, own * count + j], count)
                        total = total + weight * inbox[place, way, part].astype(F32)
                    sums.append(total)
                plus.append((sums[0] + sums[1]).astype(BF16))
                minus.append((sums[0] - sums[1]).astype(BF16))
            left = dot(operator, jnp.concatenate([plus[1], -plus[0]], axis=1))
            right = dot(jnp.concatenate([minus[1], -minus[0]], axis=0), operator)
            for part in range(2):
                lam = decay[j] * state[j, part].astype(F32)
                lam = lam + left[:, part * dim : (part + 1) * dim]
                lam = lam - right[part * dim : (part + 1) * dim]
                hist[step, 0, j, part] = lam.astype(BF16)
            return carry

        lax.fori_loop(0, count, one, 0)

    def rotate(step, half):
        def one(sub, carry):
            at = step * subs + sub
            mult_r = right_u[at]
            mult_l = left_u[at]
            for j in range(0, count, 2):
                rows = jnp.concatenate(
                    [
                        jnp.concatenate(
                            [hist[step, sub, j + i, 0], hist[step, sub, j + i, 1]], axis=1
                        )
                        for i in range(2)
                    ],
                    axis=0,
                )
                middle = dot(rows, mult_r).astype(BF16)
                stacked = jnp.concatenate(
                    [
                        jnp.concatenate([middle[:dim, :dim], middle[dim:, :dim]], axis=1),
                        jnp.concatenate([middle[:dim, dim:], middle[dim:, dim:]], axis=1),
                    ],
                    axis=0,
                )
                result = dot(mult_l, stacked).astype(BF16)
                for i in range(2):
                    for part in range(2):
                        hist[step, sub + 1, j + i, part] = result[
                            part * dim : (part + 1) * dim, i * dim : (i + 1) * dim
                        ]
            return carry

        lax.fori_loop(half * batch, (half + 1) * batch, one, 0)

    prepare()
    fill_stage(adjoint, level)
    pl.semaphore_wait(barrier, owners - 1)
    for step in range(steps):
        state = adjoint if step == 0 else hist.at[step - 1, subs]
        for way in range(2):

            @pl.when(goes_on(way, 1))
            def _(way=way):
                chain_copy(step, way, 1, state).start()

        if step > 0:
            pl.semaphore_wait(credit, lanes - 1)
            fill_stage(state, level)
        send_stage(level)
        if step == 0:
            fetch.wait()
        beside = [[] for _ in range(depth)]
        for sub in range(subs):
            beside[sub * depth // subs].append(sub)

        def aside(place):
            for sub in beside[place]:
                if step > 0:
                    project(step - 1, sub)
                if step == 0:
                    turn(sub)

        aside(0)
        for hop in range(1, depth):
            for way in range(2):

                @pl.when(arrives(way, hop))
                def _(way=way, hop=hop):
                    block = chain_block(step, way, hop)
                    chain_copy(step, way, hop, block).wait_recv()
                    if hop + 1 < depth:

                        @pl.when(goes_on(way, hop + 1))
                        def _():
                            chain_copy(step, way, hop + 1, block).start()

                    serve(block, from_level(way, hop))

            aside(hop)

        def collect(offset, carry):
            for a_level in range(depth):
                source = owner_of(lane_of(offset), a_level)
                pltpu.make_async_remote_copy(
                    src_ref=stage.at[offset - 1, a_level],
                    dst_ref=inbox.at[source],
                    send_sem=plane_send.at[offset - 1, a_level],
                    recv_sem=plane_recv.at[source],
                    device_id=lane_id(lane_of(offset)),
                    device_id_type=MESH,
                ).wait_recv()
            return carry

        lax.fori_loop(1, lanes, collect, 0)
        couple(step, state)
        if step + 1 < steps:

            def allow(offset, carry):
                pl.semaphore_signal(
                    credit, inc=1, device_id=lane_id(lane_of(offset)), device_id_type=MESH
                )
                return carry

            lax.fori_loop(1, lanes, allow, 0)
        for half in range(halves):
            rotate(step, half)
            if step == steps - 1:
                for sub in range(half * batch, (half + 1) * batch):
                    project(step, sub)
                    if sub == subs - 1:
                        result = pltpu.make_async_copy(hist.at[step, subs], out, local.at[1])
                        result.start()

        def settle(offset, carry):
            for a_level in range(depth):
                plane_copy(offset, a_level).wait_send()
            return carry

        lax.fori_loop(1, lanes, settle, 0)
        for hop in range(1, depth):
            for way in range(2):

                @pl.when(goes_on(way, hop))
                def _(way=way, hop=hop):
                    chain_copy(step, way, hop, chain_block(step, way, hop)).wait_send()

    result.wait()
    for group in range(steps * halves):
        finish(group)


def pick_kernel(owners, count, modes, higher, lower, picks):
    total = owners * count
    names = lax.broadcasted_iota(jnp.int32, (owners, total), 0)
    member = lax.div(lax.broadcasted_iota(jnp.int32, (total, owners), 0), count)
    member = (member == lax.broadcasted_iota(jnp.int32, (total, owners), 1)).astype(F32)
    for way, table in enumerate((higher, lower)):
        spread = jnp.zeros((owners, total), F32)
        for mode in range(modes):
            link = table[mode : mode + 1, :]
            source = lax.div(link, count)
            local = (link - source * count).astype(F32)
            spread = spread + jnp.where(source == names, local, 0.0)
        found = dot(spread.astype(BF16), member.astype(BF16))
        picks[way * owners : (way + 1) * owners, :] = found.astype(jnp.int32)


def body(adjoint, saved, propagators, coupling, higher, lower, ladder, rates, decay):
    nodes = lax.axis_size("node")
    cores = lax.axis_size("cores")
    owners = nodes * cores
    own = lax.axis_index(("node", "cores"))
    count = adjoint.shape[0]
    modes = higher.shape[1]
    steps, subs = propagators.shape[:2]
    dim = coupling.shape[0]
    depth = 1 << (cores.bit_length() // 2)
    width = cores // depth
    lanes = nodes * width
    rows = dim // owners
    halves = 2 if subs % 2 == 0 else 1
    batch = subs // halves
    higher, lower, ladder = higher.T, lower.T, jnp.swapaxes(ladder, 1, 2)
    smem = pl.BlockSpec(memory_space=pltpu.SMEM)
    vmem = pl.BlockSpec(memory_space=pltpu.VMEM)
    picks = pl.pallas_call(
        functools.partial(pick_kernel, owners, count, modes),
        out_shape=jax.ShapeDtypeStruct((2 * owners, owners), jnp.int32),
        in_specs=[vmem, vmem],
        out_specs=vmem,
    )(higher, lower)
    block = adjoint.shape
    hbm = pl.BlockSpec(memory_space=pl.ANY)
    hops = depth - 1
    state, grad = pl.pallas_call(
        functools.partial(kernel, (nodes, depth, width, count, modes, steps, subs, dim, halves)),
        out_shape=(
            jax.ShapeDtypeStruct(block, BF16),
            jax.ShapeDtypeStruct((rows, steps * subs, 2, dim), F32),
        ),
        in_specs=[smem] * 6 + [vmem, hbm, vmem, vmem],
        out_specs=(hbm, vmem),
        scratch_shapes=[
            pltpu.VMEM((steps * subs, 2 * dim, 2 * dim), BF16),
            pltpu.VMEM((steps * subs, 2 * dim, 2 * dim), BF16),
            pltpu.VMEM((steps, subs + 1) + block, BF16),
            pltpu.VMEM((lanes - 1, depth, 2) + block[1:], BF16),
            pltpu.VMEM((owners, 2) + block[1:], BF16),
            pltpu.VMEM((batch, dim, 2 * dim), F32),
            pltpu.VMEM((steps * halves, owners, batch * rows, 2 * dim), BF16),
            pltpu.VMEM((steps * halves, owners - 1, batch * rows, 2 * dim), BF16),
            pltpu.VMEM(saved.shape, BF16),
            pltpu.VMEM((subs, dim, count * 2 * dim), BF16),
            *[pltpu.VMEM(block, BF16) for _ in range(2 * steps * hops)],
            pltpu.SemaphoreType.DMA((steps, 2, hops)),
            pltpu.SemaphoreType.DMA((steps, 2, hops)),
            pltpu.SemaphoreType.DMA((lanes - 1, depth)),
            pltpu.SemaphoreType.DMA((owners,)),
            pltpu.SemaphoreType.DMA((steps * halves,)),
            pltpu.SemaphoreType.DMA((steps * halves,)),
            pltpu.SemaphoreType.DMA((2,)),
            pltpu.SemaphoreType.REGULAR,
        ],
        compiler_params=pltpu.CompilerParams(
            collective_id=0, has_side_effects=True, vmem_limit_bytes=63_000_000
        ),
    )(picks, higher, lower, ladder, rates, decay, adjoint, saved, propagators, coupling)
    return state, grad


def solution(mesh):
    return jax.shard_map(
        body,
        mesh=mesh,
        in_specs=(
            P(("node", "cores"), None, None, None),
            P(None, None, ("node", "cores"), None, None, None),
            P(),
            P(),
            P(),
            P(),
            P(None, ("node", "cores"), None),
            P(),
            P(("node", "cores")),
        ),
        out_specs=(P(("node", "cores"), None, None, None), P(("node", "cores"), None, None, None)),
        check_vma=False,
    )
```

profile of v0, /device:TPU:0, one launch (start us, length us, event | category | flops | bytes accessed | tf_op | source)
XLA Modules:
  0.0 135.6 jit_solution(16151542872957868212)
XLA Ops:
  0.6 1.5 %shard_map.104.picks = s32[64,32]{1,0:T(8,128)} custom-call(s32[4,256]{1,0:T(4,128)} %bitcast.3, s32[4,256]{1,0:T(4,128)} %bitcast.5), custom_call_target="tpu_custom_call" | custom-call | tf_op jit(solution)/shard_map/pallas_call | solution.py:428
  2.1 130.2 %shard_map.105 = (bf16[8,2,128,128]{3,2,1,0:T(8,128)(2,1)}, f32[4,8,2,128]{3,2,1,0:T(2,128)}) custom-call(s32[64,32]{1,0:T(8,128)} %shard_map.104.picks, s32[4,256]{1,0:T(4,128)} %bitcast.4, s32[4,256]{1,0:T(4,128)} %bitcast.6, s32[2,4,8]{2,1,0:T(4,128)} %bitcast.7, f32[2,4]{1,0:T(2,128)} %rates.1, f32[8]{0:T(128)} %decay.1, ...), custom_call_target="tpu_custom_call" | custom-call | tf_op jit(solution)/shard_map/pallas_call | solution.py:437
  132.3 1.9 %copy.13 = bf16[8,2,128,128]{3,2,1,0:T(8,128)(2,1)} copy(bf16[8,2,128,128]{3,2,1,0:T(8,128)(2,1)} %get-tuple-element.4) | data formatting | bytes 1048576
  134.2 1.4 %copy.14 = f32[4,8,2,128]{3,2,1,0:T(2,128)} copy(f32[4,8,2,128]{3,2,1,0:T(2,128)} %get-tuple-element.5) | data formatting | bytes 65536
where the time goes:
time: 136 us
  Pallas kernels  132 us (97%)
  local copies, waits for them, and re-layouts  3.26 us (2%)
    pallas_call x1, Pallas kernels, body(): pl.pallas_call(functools.partial(kernel, (nodes, depth, width, count, mod...  130 us
    unnamed x2, local copies, waits for them, and re-layouts  3.26 us

commit v1 on v0

v1 whole, which is shorter than its diff:
```python
import functools

import jax
import jax.numpy as jnp
from jax import lax
from jax.experimental import pallas as pl
from jax.experimental.pallas import tpu as pltpu
from jax.sharding import PartitionSpec as P

MESH = pl.DeviceIdType.MESH
F32 = jnp.float32
BF16 = jnp.bfloat16


def dot(a, b):
    return jnp.dot(a, b, preferred_element_type=F32)


def kernel(
    dims,
    higher,
    lower,
    ladder,
    rates,
    decay,
    adjoint,
    saved_in,
    propagators,
    coupling,
    out,
    grad,
    right_u,
    left_u,
    hist,
    zout,
    zin,
    rout,
    rin,
    terms,
    term_stage,
    term_inbox,
    saved,
    saved_t,
    place,
    weight,
    ladders,
    near_send,
    near_recv,
    near_pass,
    near_take,
    line_send,
    line_recv,
    line_pass,
    line_take,
    z_send,
    z_recv,
    r_send,
    r_recv,
    ladder_send,
    ladder_recv,
    term_send,
    term_recv,
    local,
    *gathered,
):
    nodes, depth, width, pair, count, modes, steps, subs, dim, halves, pieces = dims
    near, line = gathered[:steps], gathered[steps:]
    cores = depth * width
    owners = nodes * cores
    tall = nodes // pair
    chips = tall * width
    rows = dim // owners
    batch = subs // halves
    piece = count // pieces
    slots = 2 * modes
    node = lax.axis_index("node")
    spot = lax.axis_index("cores")
    level = spot // width
    column = spot % width
    side = node // pair
    core = node % pair
    chip = side * width + column

    def chip_id(other):
        return ((other // width) * pair + core, level * width + other % width)

    def chip_at(offset, sign):
        far = lax.rem(side + tall + sign * (offset // width), tall)
        return far * width + lax.rem(column + width + sign * (offset % width), width)

    def mate_id(turn):
        return (side * pair + lax.rem(core + turn, pair), spot)

    def level_id(other):
        return (node, other * width + column)

    barrier = pltpu.get_barrier_semaphore()

    own = node * cores + spot

    def owner_id(offset):
        other = lax.rem(own + offset, owners)
        return (other // cores, lax.rem(other, cores))

    def greet(offset, carry):
        pl.semaphore_signal(barrier, inc=1, device_id=owner_id(offset), device_id_type=MESH)
        return carry

    lax.fori_loop(1, owners, greet, 0)
    fetch = pltpu.make_async_copy(saved_in, saved, local.at[0])
    fetch.start()

    def remote(source, target, sent, arrived, device):
        return pltpu.make_async_remote_copy(
            src_ref=source,
            dst_ref=target,
            send_sem=sent,
            recv_sem=arrived,
            device_id=device,
            device_id_type=MESH,
        )

    def near_block(step, a_chip, a_core):
        return near[step].at[pl.ds((a_chip * pair + a_core) * count, count)]

    def line_block(step, a_core, a_level):
        return line[step].at[pl.ds((a_core * depth + a_level) * count, count)]

    def near_copy(step, offset, source):
        return remote(
            source,
            near_block(step, chip, core),
            near_send.at[step, offset - 1],
            near_recv.at[step, offset - 1],
            chip_id(chip_at(offset, 1)),
        )

    def near_mate(step, a_chip, turn, source):
        return remote(
            source,
            near_block(step, a_chip, core),
            near_pass.at[step, turn - 1, a_chip],
            near_take.at[step, turn - 1, a_chip],
            mate_id(turn),
        )

    def line_copy(step, way, hop, source):
        a_level = level - (hop - 1) if way == 0 else level + (hop - 1)
        return remote(
            source,
            line_block(step, core, a_level),
            line_send.at[step, way, hop - 1],
            line_recv.at[step, way, hop - 1],
            level_id(level + 1 if way == 0 else level - 1),
        )

    def line_mate(step, a_level, turn, source):
        return remote(
            source,
            line_block(step, core, a_level),
            line_pass.at[step, turn - 1, a_level],
            line_take.at[step, turn - 1, a_level],
            mate_id(turn),
        )

    def z_copy(step, way, a_level, k):
        return remote(
            zout.at[step, a_level, pl.ds(k * piece, piece)],
            zin.at[step, way, a_level, pl.ds(k * piece, piece)],
            z_send.at[step, a_level, k],
            z_recv.at[step, way, a_level, k],
            level_id(level + 1 if way == 0 else level - 1),
        )

    def r_copy(step, offset):
        target = chip_at(offset, 1)
        return remote(
            rout.at[step, target],
            rin.at[step, offset - 1],
            r_send.at[step, offset - 1],
            r_recv.at[step, offset - 1],
            chip_id(target),
        )

    def ladder_level(other):
        return remote(
            ladder, ladders.at[level], ladder_send.at[other], ladder_recv.at[level], level_id(other)
        )

    def ladder_chip(other):
        return remote(
            ladder,
            ladders.at[depth + chip],
            ladder_send.at[depth + other],
            ladder_recv.at[depth + chip],
            chip_id(other),
        )

    def each_ladder(act):
        def one_level(other, carry):
            @pl.when(other != level)
            def _():
                act(ladder_level(other))

            return carry

        def one_chip(other, carry):
            @pl.when(other != chip)
            def _():
                act(ladder_chip(other))

            return carry

        lax.fori_loop(0, depth, one_level, 0)
        lax.fori_loop(0, chips, one_chip, 0)

    def take_ladders():
        def one_level(other, carry):
            @pl.when(other != level)
            def _():
                remote(
                    ladder,
                    ladders.at[other],
                    ladder_send.at[other],
                    ladder_recv.at[other],
                    level_id(other),
                ).wait_recv()

            return carry

        def one_chip(other, carry):
            @pl.when(other != chip)
            def _():
                remote(
                    ladder,
                    ladders.at[depth + other],
                    ladder_send.at[depth + other],
                    ladder_recv.at[depth + other],
                    chip_id(other),
                ).wait_recv()

            return carry

        lax.fori_loop(0, depth, one_level, 0)
        lax.fori_loop(0, chips, one_chip, 0)

    def tabulate():
        for way in range(2):
            for mode in range(modes):
                for j in range(count):
                    value = ladder[way, mode, j]
                    ladders[level, way, mode, j] = value
                    ladders[depth + chip, way, mode, j] = value

        def entry(at, along_z):
            index, j = at // count, at % count
            if along_z:
                target = node * cores + index * width + column
            else:
                target = ((index // width) * pair + core) * cores + level * width + index % width
            row = index if along_z else depth + index
            for way in range(2):
                for mode in range(modes):
                    link = (higher, lower)[way][mode, target * count + j]
                    source = link // count
                    a_node, a_spot = source // cores, source % cores
                    a_level, a_column = a_spot // width, a_spot % width
                    a_side, a_core = a_node // pair, a_node % pair
                    if along_z:
                        here = a_level == level
                        block = (a_side * width + a_column) * pair + a_core
                    else:
                        here = jnp.logical_and(a_side == side, a_column == column)
                        block = a_core * depth + a_level
                    value = ladders[row, way, mode, j].astype(F32) * rates[way, mode]
                    spot_at = ((row * count + j) * 2 + way) * modes + mode
                    place[spot_at] = block * count + link % count
                    weight[spot_at] = jnp.where(here, value, 0.0)

        def entry_z(at, carry):
            entry(at, True)
            return carry

        def entry_r(at, carry):
            entry(at, False)
            return carry

        lax.fori_loop(0, depth * count, entry_z, 0)
        lax.fori_loop(0, chips * count, entry_r, 0)

    def partial(blocks, row, put):
        operator = coupling[...]

        def some(pick, carry):
            plus, minus = [], []
            for i in range(2):
                sums = []
                for way in range(2):
                    total = None
                    for mode in range(modes):
                        at = ((row * count + pick * 2 + i) * 2 + way) * modes + mode
                        scale = jnp.full((16, dim), weight[at], F32).astype(BF16)
                        term = blocks[place[at]].reshape(dim // 16, 16, dim) * scale
                        total = term if total is None else total + term
                    sums.append(total.reshape(dim, dim))
                plus.append(sums[0] + sums[1])
                minus.append(sums[0] - sums[1])
            left = dot(operator, jnp.concatenate(plus, axis=1))
            right = dot(jnp.concatenate(minus, axis=0), operator)
            for i in range(2):
                value = left[:, i * dim : (i + 1) * dim] - right[i * dim : (i + 1) * dim]
                put(pick * 2 + i, value.astype(BF16))
            return carry

        lax.fori_loop(0, count // 2, some, 0)

    def prepare():
        def one(at, carry):
            step, sub = at // subs, at % subs
            u_re = propagators[step, sub, 0]
            u_im = propagators[step, sub, 1]
            right_u[at, :dim, :dim] = u_re
            right_u[at, :dim, dim:] = u_im
            right_u[at, dim:, :dim] = -u_im
            right_u[at, dim:, dim:] = u_re
            t_re = u_re.T
            t_im = u_im.T
            left_u[at, :dim, :dim] = t_re
            left_u[at, :dim, dim:] = t_im
            left_u[at, dim:, :dim] = -t_im
            left_u[at, dim:, dim:] = t_re
            return carry

        lax.fori_loop(0, steps * subs, one, 0)

    def turn_saved(sub):
        for j in range(count):
            kept = saved[steps - 1, sub, j].reshape(2 * dim, dim)
            saved_t[sub, :, 2 * dim * j : 2 * dim * (j + 1)] = kept.T

    def project(step, sub):
        total = jnp.zeros((dim, 2 * dim), F32)
        for j in range(count):
            lam_re = hist[step, sub + 1, j, 0]
            lam_im = hist[step, sub + 1, j, 1]
            both = jnp.concatenate(
                [
                    jnp.concatenate([lam_re, lam_im], axis=1),
                    jnp.concatenate([lam_im, -lam_re], axis=1),
                ],
                axis=0,
            )
            if step == steps - 1:
                kept_t = saved_t[sub, :, 2 * dim * j : 2 * dim * (j + 1)]
                total = total + dot(kept_t, both)
            else:
                kept = saved[step, sub, j].reshape(2 * dim, dim)
                total = total + lax.dot_general(
                    kept, both, (((0,), (0,)), ((), ())), preferred_element_type=F32
                )
        terms[sub % batch] = total
        if sub % batch == batch - 1:
            spread(step * halves + sub // batch)

    def spread(group):
        for target in range(owners):
            term_stage[group, target] = jnp.concatenate(
                [terms[i, target * rows : (target + 1) * rows] for i in range(batch)], axis=0
            ).astype(BF16)

        def send(offset, carry):
            pltpu.make_async_remote_copy(
                src_ref=term_stage.at[group, lax.rem(own + offset, owners)],
                dst_ref=term_inbox.at[group, offset - 1],
                send_sem=term_send.at[group],
                recv_sem=term_recv.at[group],
                device_id=owner_id(offset),
                device_id_type=MESH,
            ).start()
            return carry

        lax.fori_loop(1, owners, send, 0)

    def finish(group):
        everything = term_inbox.at[group]
        pltpu.make_async_copy(everything, everything, term_recv.at[group]).wait()
        total = term_stage[group, own].astype(F32)
        for offset in range(1, owners):
            total = total + term_inbox[group, offset - 1].astype(F32)
        for i in range(batch):
            for row in range(rows):
                for part in range(2):
                    grad[row, group * batch + i, part : part + 1, :] = total[
                        i * rows + row : i * rows + row + 1, part * dim : (part + 1) * dim
                    ]
        pltpu.make_async_copy(everything, everything, term_send.at[group]).wait()

    def rotate(step, half):
        def one(sub, carry):
            at = step * subs + sub
            mult_r = right_u[at]
            mult_l = left_u[at]
            for j in range(0, count, 2):
                rows = jnp.concatenate(
                    [
                        jnp.concatenate(
                            [hist[step, sub, j + i, 0], hist[step, sub, j + i, 1]], axis=1
                        )
                        for i in range(2)
                    ],
                    axis=0,
                )
                middle = dot(rows, mult_r).astype(BF16)
                stacked = jnp.concatenate(
                    [
                        jnp.concatenate([middle[:dim, :dim], middle[dim:, :dim]], axis=1),
                        jnp.concatenate([middle[:dim, dim:], middle[dim:, dim:]], axis=1),
                    ],
                    axis=0,
                )
                result = dot(mult_l, stacked).astype(BF16)
                for i in range(2):
                    for part in range(2):
                        hist[step, sub + 1, j + i, part] = result[
                            part * dim : (part + 1) * dim, i * dim : (i + 1) * dim
                        ]
            return carry

        lax.fori_loop(half * batch, (half + 1) * batch, one, 0)

    def join(step, state):
        def one(j, carry):
            lam = decay[j] * state[j, 0].astype(F32) + zout[step, level, j].astype(F32)
            hist[step, 0, j, 0] = lam.astype(BF16)
            total = rout[step, chip, j].astype(F32)
            for offset in range(1, chips):
                total = total + rin[step, offset - 1, j].astype(F32)
            lam = decay[j] * state[j, 1].astype(F32) - total
            hist[step, 0, j, 1] = lam.astype(BF16)
            return carry

        lax.fori_loop(0, count, one, 0)

    def arrives(way, hop):
        return level >= hop if way == 0 else level + hop < depth

    def goes_on(way, hop):
        if way == 0:
            return jnp.logical_and(level >= hop - 1, level < depth - 1)
        return jnp.logical_and(level + hop - 1 < depth, level > 0)

    def take_line(step, hop):
        for way in range(2):

            @pl.when(arrives(way, hop))
            def _(way=way):
                a_level = level - hop if way == 0 else level + hop
                block = line_block(step, core, a_level)
                remote(
                    block,
                    block,
                    line_send.at[step, way, hop - 1],
                    line_recv.at[step, way, hop - 1],
                    level_id(level),
                ).wait_recv()
                if hop + 1 < depth:

                    @pl.when(goes_on(way, hop + 1))
                    def _():
                        line_copy(step, way, hop + 1, block).start()

                for turn in range(1, pair):
                    line_mate(step, a_level, turn, block).start()

    def take_near(step):
        def one(offset, carry):
            a_chip = chip_at(offset, -1)
            block = near_block(step, a_chip, core)
            near_copy(step, offset, block).wait_recv()
            for turn in range(1, pair):
                near_mate(step, a_chip, turn, block).start()
            return carry

        lax.fori_loop(1, chips, one, 0)
        for turn in range(1, pair):

            def two(a_chip, carry, turn=turn):
                block = near_block(step, a_chip, lax.rem(core + pair - turn, pair))
                near_mate(step, a_chip, turn, block).wait_recv()
                return carry

            lax.fori_loop(0, chips, two, 0)

    def mates_line(step):
        for turn in range(1, pair):

            def two(a_level, carry, turn=turn):
                block = line_block(step, lax.rem(core + pair - turn, pair), a_level)
                line_mate(step, a_level, turn, block).wait_recv()
                return carry

            lax.fori_loop(0, depth, two, 0)

    def reduce_start(step):
        def one(i, carry):
            a_level = jnp.where(level * 2 < depth, depth - 1 - i, i)

            def put(j, value):
                zout[step, a_level, j] = value

            partial(near[step], a_level, put)

            def send(way):
                for k in range(pieces):
                    z_copy(step, way, a_level, k).start()

            pl.when(jnp.logical_and(level == 0, a_level > 0))(lambda: send(0))
            pl.when(jnp.logical_and(level == depth - 1, a_level < depth - 1))(lambda: send(1))
            return carry

        lax.fori_loop(0, depth, one, 0)

    def exchange(step):
        def one(i, carry):
            offset = lax.rem(i + 1, chips)
            target = chip_at(offset, 1)

            def put(j, value):
                rout[step, target, j] = value

            partial(line[step], depth + target, put)

            @pl.when(offset > 0)
            def _():
                r_copy(step, offset).start()

            return carry

        lax.fori_loop(0, chips, one, 0)

    def reduce_on(step):
        for ahead in range(max(depth - 2, 0), -1, -1):
            for k in range(pieces):
                for way in range(2):
                    if way == 0:
                        a_level = level + ahead
                        fits = jnp.logical_and(level > 0, a_level < depth)
                    else:
                        a_level = level - ahead
                        fits = jnp.logical_and(level < depth - 1, a_level >= 0)

                    @pl.when(fits)
                    def _(way=way, k=k, a_level=a_level):
                        z_copy(step, way, a_level, k).wait_recv()
                        for j in range(k * piece, (k + 1) * piece):
                            total = zout[step, a_level, j].astype(F32)
                            total = total + zin[step, way, a_level, j].astype(F32)
                            zout[step, a_level, j] = total.astype(BF16)
                        if ahead > 0:
                            z_copy(step, way, a_level, k).start()

    prepare()
    pl.semaphore_wait(barrier, owners - 1)
    for step in range(steps):
        state = adjoint if step == 0 else hist.at[step - 1, subs]
        re, im = state.at[:, 0], state.at[:, 1]
        for way in range(2):

            @pl.when(goes_on(way, 1))
            def _(way=way):
                line_copy(step, way, 1, re).start()

        def plane(offset, carry, step=step, im=im):
            near_copy(step, offset, im).start()
            return carry

        lax.fori_loop(1, chips, plane, 0)
        for turn in range(1, pair):
            near_mate(step, chip, turn, im).start()
            line_mate(step, level, turn, re).start()
        keep_im = pltpu.make_async_copy(im, near_block(step, chip, core), local.at[2])
        keep_re = pltpu.make_async_copy(re, line_block(step, core, level), local.at[3])
        keep_im.start()
        keep_re.start()
        if step == 0:
            each_ladder(lambda copy: copy.start())
            fetch.wait()
            for sub in range(subs):
                turn_saved(sub)
            take_ladders()
            tabulate()
        else:
            for sub in range(subs):
                project(step - 1, sub)
        if depth > 1:
            take_line(step, 1)
        keep_im.wait()
        keep_re.wait()
        take_near(step)
        if depth > 2:
            take_line(step, 2)
        reduce_start(step)
        for hop in range(3, depth):
            take_line(step, hop)
        mates_line(step)
        exchange(step)
        reduce_on(step)

        def collect(offset, carry, step=step):
            r_copy(step, offset).wait_recv()
            return carry

        lax.fori_loop(1, chips, collect, 0)
        join(step, state)
        for half in range(halves):
            rotate(step, half)
            if step == steps - 1:
                for sub in range(half * batch, (half + 1) * batch):
                    project(step, sub)
                    if sub == subs - 1:
                        result = pltpu.make_async_copy(hist.at[step, subs], out, local.at[1])
                        result.start()

        for hop in range(1, depth):
            for way in range(2):

                @pl.when(goes_on(way, hop))
                def _(way=way, hop=hop):
                    a_level = level - (hop - 1) if way == 0 else level + (hop - 1)
                    line_copy(step, way, hop, line_block(step, core, a_level)).wait_send()

        def done_chip(offset, carry, step=step):
            near_copy(step, offset, near_block(step, chip, core)).wait_send()
            r_copy(step, offset).wait_send()
            return carry

        lax.fori_loop(1, chips, done_chip, 0)
        for turn in range(1, pair):

            def done_near(a_chip, carry, step=step, turn=turn):
                near_mate(step, a_chip, turn, near_block(step, a_chip, core)).wait_send()
                return carry

            def done_line(a_level, carry, step=step, turn=turn):
                line_mate(step, a_level, turn, line_block(step, core, a_level)).wait_send()
                return carry

            lax.fori_loop(0, chips, done_near, 0)
            lax.fori_loop(0, depth, done_line, 0)

        def done_z(a_level, carry, step=step):
            @pl.when(a_level != level)
            def _():
                for k in range(pieces):
                    z_copy(step, 0, a_level, k).wait_send()

            return carry

        lax.fori_loop(0, depth, done_z, 0)

    each_ladder(lambda copy: copy.wait_send())
    result.wait()
    for group in range(steps * halves):
        finish(group)


def body(adjoint, saved, propagators, coupling, higher, lower, ladder, rates, decay):
    nodes = lax.axis_size("node")
    cores = lax.axis_size("cores")
    owners = nodes * cores
    count = adjoint.shape[0]
    modes = higher.shape[1]
    steps, subs = propagators.shape[:2]
    dim = coupling.shape[0]
    depth = 1 << (cores.bit_length() // 2)
    width = cores // depth
    pair = 2 if nodes % 2 == 0 else 1
    chips = nodes // pair * width
    pieces = 2
    rows = dim // owners
    halves = 2 if subs % 2 == 0 else 1
    batch = subs // halves
    higher, lower, ladder = higher.T, lower.T, jnp.swapaxes(ladder, 1, 2)
    smem = pl.BlockSpec(memory_space=pltpu.SMEM)
    vmem = pl.BlockSpec(memory_space=pltpu.VMEM)
    block = adjoint.shape
    hbm = pl.BlockSpec(memory_space=pl.ANY)
    hops = max(depth - 1, 1)
    others = max(chips - 1, 1)
    mates = max(pair - 1, 1)
    half = (count,) + block[2:]
    table = (depth + chips) * count * 2 * modes
    dma = pltpu.SemaphoreType.DMA
    state, grad = pl.pallas_call(
        functools.partial(kernel, (nodes, depth, width, pair, count, modes, steps, subs, dim, halves, pieces)),
        out_shape=(
            jax.ShapeDtypeStruct(block, BF16),
            jax.ShapeDtypeStruct((rows, steps * subs, 2, dim), F32),
        ),
        in_specs=[smem] * 5 + [vmem, hbm, vmem, vmem],
        out_specs=(hbm, vmem),
        scratch_shapes=[
            pltpu.VMEM((steps * subs, 2 * dim, 2 * dim), BF16),
            pltpu.VMEM((steps * subs, 2 * dim, 2 * dim), BF16),
            pltpu.VMEM((steps, subs + 1) + block, BF16),
            pltpu.VMEM((steps, depth) + half, BF16),
            pltpu.VMEM((steps, 2, depth) + half, BF16),
            pltpu.VMEM((steps, chips) + half, BF16),
            pltpu.VMEM((steps, others) + half, BF16),
            pltpu.VMEM((batch, dim, 2 * dim), F32),
            pltpu.VMEM((steps * halves, owners, batch * rows, 2 * dim), BF16),
            pltpu.VMEM((steps * halves, owners - 1, batch * rows, 2 * dim), BF16),
            pltpu.VMEM(saved.shape, BF16),
            pltpu.VMEM((subs, dim, count * 2 * dim), BF16),
            pltpu.SMEM((table,), jnp.int32),
            pltpu.SMEM((table,), F32),
            pltpu.SMEM((depth + chips, 2, modes, count), jnp.int32),
            dma((steps, others)),
            dma((steps, others)),
            dma((steps, mates, chips)),
            dma((steps, mates, chips)),
            dma((steps, 2, hops)),
            dma((steps, 2, hops)),
            dma((steps, mates, depth)),
            dma((steps, mates, depth)),
            dma((steps, depth, pieces)),
            dma((steps, 2, depth, pieces)),
            dma((steps, others)),
            dma((steps, others)),
            dma((depth + chips,)),
            dma((depth + chips,)),
            dma((steps * halves,)),
            dma((steps * halves,)),
            dma((4,)),
            *[pltpu.VMEM((chips * pair * count, dim, dim), BF16)] * steps,
            *[pltpu.VMEM((depth * pair * count, dim, dim), BF16)] * steps,
        ],
        compiler_params=pltpu.CompilerParams(
            collective_id=0, has_side_effects=True, vmem_limit_bytes=63_000_000
        ),
    )(higher, lower, ladder, rates, decay, adjoint, saved, propagators, coupling)
    return state, grad


def solution(mesh):
    return jax.shard_map(
        body,
        mesh=mesh,
        in_specs=(
            P(("node", "cores"), None, None, None),
            P(None, None, ("node", "cores"), None, None, None),
            P(),
            P(),
            P(),
            P(),
            P(None, ("node", "cores"), None),
            P(),
            P(("node", "cores")),
        ),
        out_specs=(P(("node", "cores"), None, None, None), P(("node", "cores"), None, None, None)),
        check_vma=False,
    )
```

time: 136 us -> 124 us (0.912)
  Pallas kernels: 132 us -> 120 us
    pallas_call x2 -> x1, Pallas kernels: 132 us -> 120 us  [body(): pl.pallas_call(functools.partial(kernel, (nodes, depth, width, pair, coun...]
where the time goes in v1:
time: 124 us; the launch traced here: 123 us
  Pallas kernels  120 us (97%)
  local copies, waits for them, and re-layouts  3.26 us (3%)
    pallas_call x1, Pallas kernels, body(): pl.pallas_call(functools.partial(kernel, (nodes, depth, width, pair, coun...  120 us
    unnamed x2, local copies, waits for them, and re-layouts  3.26 us

profile of v1, /device:TPU:0, one launch (start us, length us, event | category | flops | bytes accessed | tf_op | source)
XLA Modules:
  0.0 123.5 jit_solution(836220537879375145)
XLA Ops:
  0.6 119.6 %shard_map.104 = (bf16[8,2,128,128]{3,2,1,0:T(8,128)(2,1)}, f32[4,8,2,128]{3,2,1,0:T(2,128)}) custom-call(s32[4,256]{1,0:T(4,128)} %bitcast.3, s32[4,256]{1,0:T(4,128)} %bitcast.4, s32[2,4,8]{2,1,0:T(4,128)} %bitcast.5, f32[2,4]{1,0:T(2,128)} %rates.1, f32[8]{0:T(128)} %decay.1, bf16[8,2,128,128]{3,2,1,0:T(8,128)(2,1)} %adjoint.1, ...), custom_call_target="tpu_custom_call" | custom-call | tf_op jit(solution)/shard_map/pallas_call | solution.py:694
  120.2 1.9 %copy.13 = bf16[8,2,128,128]{3,2,1,0:T(8,128)(2,1)} copy(bf16[8,2,128,128]{3,2,1,0:T(8,128)(2,1)} %get-tuple-element.4) | data formatting | bytes 1048576
  122.1 1.4 %copy.14 = f32[4,8,2,128]{3,2,1,0:T(2,128)} copy(f32[4,8,2,128]{3,2,1,0:T(2,128)} %get-tuple-element.5) | data formatting | bytes 65536

commit v2 on v1

--- a/solution.py
+++ b/solution.py
@@ -35,7 +35,10 @@
     zout,
     zin,
     rout,
-    rin,
+    row_in,
+    col_in,
+    row_end,
+    col_end,
     terms,
     term_stage,
     term_inbox,
@@ -43,6 +46,8 @@
     saved_t,
     place,
     weight,
+    home,
+    inside,
     ladders,
     near_send,
     near_recv,
@@ -54,8 +59,14 @@
     line_take,
     z_send,
     z_recv,
-    r_send,
-    r_recv,
+    row_send,
+    row_recv,
+    col_send,
+    col_recv,
+    row_last,
+    row_done,
+    col_last,
+    col_done,
     ladder_send,
     ladder_recv,
     term_send,
@@ -81,12 +92,16 @@
     core = node % pair
     chip = side * width + column
 
+    def split(value, size):
+        if size & (size - 1) == 0:
+            return value >> (size.bit_length() - 1), value & (size - 1)
+        return lax.div(value, size), lax.rem(value, size)
+
     def chip_id(other):
         return ((other // width) * pair + core, level * width + other % width)
 
-    def chip_at(offset, sign):
-        far = lax.rem(side + tall + sign * (offset // width), tall)
-        return far * width + lax.rem(column + width + sign * (offset % width), width)
+    def chip_at(up, right):
+        return lax.rem(side + up + tall, tall) * width + lax.rem(column + right + width, width)
 
     def mate_id(turn):
         return (side * pair + lax.rem(core + turn, pair), spot)
@@ -120,46 +135,58 @@
             device_id_type=MESH,
         )
 
-    def near_block(step, a_chip, a_core):
-        return near[step].at[pl.ds((a_chip * pair + a_core) * count, count)]
-
-    def line_block(step, a_core, a_level):
-        return line[step].at[pl.ds((a_core * depth + a_level) * count, count)]
-
-    def near_copy(step, offset, source):
+    def part(k):
+        return pl.ds(k * piece, piece)
+
+    def near_block(step, a_chip, a_core, k):
+        return near[step].at[pl.ds((a_chip * pair + a_core) * count + k * piece, piece)]
+
+    def line_block(step, a_core, a_level, k):
+        return line[step].at[pl.ds((a_core * depth + a_level) * count + k * piece, piece)]
+
+    def near_copy(step, up, right, k, source, a_chip, target):
+        at = up * width + right - 1
         return remote(
             source,
-            near_block(step, chip, core),
-            near_send.at[step, offset - 1],
-            near_recv.at[step, offset - 1],
-            chip_id(chip_at(offset, 1)),
-        )
-
-    def near_mate(step, a_chip, turn, source):
+            near_block(step, a_chip, core, k),
+            near_send.at[step, at, k],
+            near_recv.at[step, at, k],
+            chip_id(target),
+        )
+
+    def near_got(step, up, right, k):
+        a_chip = chip_at(-up, -right)
+        block = near_block(step, a_chip, core, k)
+        near_copy(step, up, right, k, block, a_chip, a_chip).wait_recv()
+        for turn in range(1, pair):
+            near_mate(step, a_chip, turn, k, block).start()
+        return block, a_chip
+
+    def near_mate(step, a_chip, turn, k, source):
         return remote(
             source,
-            near_block(step, a_chip, core),
-            near_pass.at[step, turn - 1, a_chip],
-            near_take.at[step, turn - 1, a_chip],
+            near_block(step, a_chip, core, k),
+            near_pass.at[step, turn - 1, a_chip, k],
+            near_take.at[step, turn - 1, a_chip, k],
             mate_id(turn),
         )
 
-    def line_copy(step, way, hop, source):
+    def line_copy(step, way, hop, k, source):
         a_level = level - (hop - 1) if way == 0 else level + (hop - 1)
         return remote(
             source,
-            line_block(step, core, a_level),
-            line_send.at[step, way, hop - 1],
-            line_recv.at[step, way, hop - 1],
+            line_block(step, core, a_level, k),
+            line_send.at[step, way, hop - 1, k],
+            line_recv.at[step, way, hop - 1, k],
             level_id(level + 1 if way == 0 else level - 1),
         )
 
-    def line_mate(step, a_level, turn, source):
+    def line_mate(step, a_level, turn, k, source):
         return remote(
             source,
-            line_block(step, core, a_level),
-            line_pass.at[step, turn - 1, a_level],
-            line_take.at[step, turn - 1, a_level],
+            line_block(step, core, a_level, k),
+            line_pass.at[step, turn - 1, a_level, k],
+            line_take.at[step, turn - 1, a_level, k],
             mate_id(turn),
         )
 
@@ -172,14 +199,40 @@
             level_id(level + 1 if way == 0 else level - 1),
         )
 
-    def r_copy(step, offset):
-        target = chip_at(offset, 1)
-        return remote(
-            rout.at[step, target],
-            rin.at[step, offset - 1],
-            r_send.at[step, offset - 1],
-            r_recv.at[step, offset - 1],
-            chip_id(target),
+    def row_copy(step, up, right):
+        return remote(
+            rout.at[step, chip_at(up, right), part(0)],
+            row_in.at[step, right - 1, up],
+            row_send.at[step, right - 1, up],
+            row_recv.at[step, right - 1, up],
+            chip_id(chip_at(0, right)),
+        )
+
+    def col_copy(step, up, right):
+        return remote(
+            rout.at[step, chip_at(up, right), part(1)],
+            col_in.at[step, up - 1, right],
+            col_send.at[step, up - 1, right],
+            col_recv.at[step, up - 1, right],
+            chip_id(chip_at(up, 0)),
+        )
+
+    def col_final(step, up):
+        return remote(
+            rout.at[step, chip_at(up, 0), part(0)],
+            col_end.at[step, up - 1],
+            col_last.at[step, up - 1],
+            col_done.at[step, up - 1],
+            chip_id(chip_at(up, 0)),
+        )
+
+    def row_final(step, right):
+        return remote(
+            rout.at[step, chip_at(0, right), part(1)],
+            row_end.at[step, right - 1],
+            row_last.at[step, right - 1],
+            row_done.at[step, right - 1],
+            chip_id(chip_at(0, right)),
         )
 
     def ladder_level(other):
@@ -252,30 +305,34 @@
                     ladders[level, way, mode, j] = value
                     ladders[depth + chip, way, mode, j] = value
 
+        def locate(owner, carry):
+            a_node, a_spot = split(owner, cores)
+            a_level, a_column = split(a_spot, width)
+            a_side, a_core = split(a_node, pair)
+            home[0, owner] = ((a_side * width + a_column) * pair + a_core) * count
+            home[1, owner] = (a_core * depth + a_level) * count
+            inside[0, owner] = jnp.where(a_level == level, 1.0, 0.0)
+            beside = jnp.logical_and(a_side == side, a_column == column)
+            inside[1, owner] = jnp.where(beside, 1.0, 0.0)
+            return carry
+
+        lax.fori_loop(0, owners, locate, 0)
+
         def entry(at, along_z):
-            index, j = at // count, at % count
+            index, j = split(at, count)
             if along_z:
-                target = node * cores + index * width + column
+                target, kind, row = node * cores + index * width + column, 0, index
             else:
-                target = ((index // width) * pair + core) * cores + level * width + index % width
-            row = index if along_z else depth + index
+                a_side, a_column = split(index, width)
+                target = (a_side * pair + core) * cores + level * width + a_column
+                kind, row = 1, depth + index
             for way in range(2):
                 for mode in range(modes):
-                    link = (higher, lower)[way][mode, target * count + j]
-                    source = link // count
-                    a_node, a_spot = source // cores, source % cores
-                    a_level, a_column = a_spot // width, a_spot % width
-                    a_side, a_core = a_node // pair, a_node % pair
-                    if along_z:
-                        here = a_level == level
-                        block = (a_side * width + a_column) * pair + a_core
-                    else:
-                        here = jnp.logical_and(a_side == side, a_column == column)
-                        block = a_core * depth + a_level
+                    source, member = split((higher, lower)[way][mode, target * count + j], count)
                     value = ladders[row, way, mode, j].astype(F32) * rates[way, mode]
-                    spot_at = ((row * count + j) * 2 + way) * modes + mode
-                    place[spot_at] = block * count + link % count
-                    weight[spot_at] = jnp.where(here, value, 0.0)
+                    slot = (row * count + j) * slots + way * modes + mode
+                    place[slot] = home[kind, source] + member
+                    weight[slot] = inside[kind, source] * value
 
         def entry_z(at, carry):
             entry(at, True)
@@ -298,7 +355,7 @@
                 for way in range(2):
                     total = None
                     for mode in range(modes):
-                        at = ((row * count + pick * 2 + i) * 2 + way) * modes + mode
+                        at = (row * count + pick * 2 + i) * slots + way * modes + mode
                         scale = jnp.full((16, dim), weight[at], F32).astype(BF16)
                         term = blocks[place[at]].reshape(dim // 16, 16, dim) * scale
                         total = term if total is None else total + term
@@ -433,13 +490,18 @@
             lam = decay[j] * state[j, 0].astype(F32) + zout[step, level, j].astype(F32)
             hist[step, 0, j, 0] = lam.astype(BF16)
             total = rout[step, chip, j].astype(F32)
-            for offset in range(1, chips):
-                total = total + rin[step, offset - 1, j].astype(F32)
             lam = decay[j] * state[j, 1].astype(F32) - total
             hist[step, 0, j, 1] = lam.astype(BF16)
             return carry
 
         lax.fori_loop(0, count, one, 0)
+
+    def fold(target, sources):
+        for j in range(piece):
+            total = target[j].astype(F32)
+            for source in sources:
+                total = total + source[j].astype(F32)
+            target[j] = total.astype(BF16)
 
     def arrives(way, hop):
         return level >= hop if way == 0 else level + hop < depth
@@ -449,59 +511,93 @@
             return jnp.logical_and(level >= hop - 1, level < depth - 1)
         return jnp.logical_and(level + hop - 1 < depth, level > 0)
 
-    def take_line(step, hop):
+    def take_line(step, hop, k):
         for way in range(2):
 
             @pl.when(arrives(way, hop))
             def _(way=way):
                 a_level = level - hop if way == 0 else level + hop
-                block = line_block(step, core, a_level)
+                block = line_block(step, core, a_level, k)
                 remote(
                     block,
                     block,
-                    line_send.at[step, way, hop - 1],
-                    line_recv.at[step, way, hop - 1],
+                    line_send.at[step, way, hop - 1, k],
+                    line_recv.at[step, way, hop - 1, k],
                     level_id(level),
                 ).wait_recv()
                 if hop + 1 < depth:
 
                     @pl.when(goes_on(way, hop + 1))
                     def _():
-                        line_copy(step, way, hop + 1, block).start()
+                        line_copy(step, way, hop + 1, k, block).start()
 
                 for turn in range(1, pair):
-                    line_mate(step, a_level, turn, block).start()
-
-    def take_near(step):
-        def one(offset, carry):
-            a_chip = chip_at(offset, -1)
-            block = near_block(step, a_chip, core)
-            near_copy(step, offset, block).wait_recv()
-            for turn in range(1, pair):
-                near_mate(step, a_chip, turn, block).start()
-            return carry
-
-        lax.fori_loop(1, chips, one, 0)
+                    line_mate(step, a_level, turn, k, block).start()
+
+    def each(lo, hi, act):
+        def one(i, carry):
+            act(i)
+            return carry
+
+        lax.fori_loop(lo, hi, one, 0)
+
+    def take_first(step):
+        def along(right):
+            block, a_chip = near_got(step, 0, right, 0)
+            each(
+                1,
+                tall,
+                lambda up: near_copy(
+                    step, up, right, 0, block, a_chip, chip_at(up, 0)
+                ).start(),
+            )
+
+        def across(up):
+            block, a_chip = near_got(step, up, 0, 1)
+            each(
+                1,
+                width,
+                lambda right: near_copy(
+                    step, up, right, 1, block, a_chip, chip_at(0, right)
+                ).start(),
+            )
+
+        each(1, width, along)
+        each(1, tall, across)
+
+    def take_second(step):
+        each(1, width, lambda right: near_got(step, 0, right, 1) and None)
+        each(1, tall, lambda up: near_got(step, up, 0, 0) and None)
+
+    def take_far(step):
+        def one(up):
+            def two(right):
+                for k in range(pieces):
+                    near_got(step, up, right, k)
+
+            each(1, width, two)
+
+        each(1, tall, one)
         for turn in range(1, pair):
 
-            def two(a_chip, carry, turn=turn):
-                block = near_block(step, a_chip, lax.rem(core + pair - turn, pair))
-                near_mate(step, a_chip, turn, block).wait_recv()
-                return carry
-
-            lax.fori_loop(0, chips, two, 0)
+            def two(a_chip, turn=turn):
+                for k in range(pieces):
+                    block = near_block(step, a_chip, lax.rem(core + pair - turn, pair), k)
+                    near_mate(step, a_chip, turn, k, block).wait_recv()
+
+            each(0, chips, two)
 
     def mates_line(step):
         for turn in range(1, pair):
 
-            def two(a_level, carry, turn=turn):
-                block = line_block(step, lax.rem(core + pair - turn, pair), a_level)
-                line_mate(step, a_level, turn, block).wait_recv()
-                return carry
-
-            lax.fori_loop(0, depth, two, 0)
-
-    def reduce_start(step):
+            def two(a_level, turn=turn):
+                for k in range(pieces):
+                    block = line_block(step, lax.rem(core + pair - turn, pair), a_level, k)
+                    line_mate(step, a_level, turn, k, block).wait_recv()
+
+            each(0, depth, two)
+
+    def reduce_start(step, lo, hi):
         def one(i, carry):
             a_level = jnp.where(level * 2 < depth, depth - 1 - i, i)
 
@@ -518,25 +614,65 @@
             pl.when(jnp.logical_and(level == depth - 1, a_level < depth - 1))(lambda: send(1))
             return carry
 
-        lax.fori_loop(0, depth, one, 0)
+        lax.fori_loop(lo, hi, one, 0)
 
     def exchange(step):
-        def one(i, carry):
-            offset = lax.rem(i + 1, chips)
-            target = chip_at(offset, 1)
+        def one(i):
+            up, right = split(chips - 1 - i, width)
+            target = chip_at(up, right)
 
             def put(j, value):
                 rout[step, target, j] = value
 
             partial(line[step], depth + target, put)
 
-            @pl.when(offset > 0)
+            @pl.when(right > 0)
             def _():
-                r_copy(step, offset).start()
-
-            return carry
-
-        lax.fori_loop(0, chips, one, 0)
+                row_copy(step, up, right).start()
+
+            @pl.when(up > 0)
+            def _():
+                col_copy(step, up, right).start()
+
+        each(0, chips, one)
+
+    def exchange_on(step):
+        def column(up):
+            target = chip_at(up, 0)
+            each(1, width, lambda right: row_copy(step, up, right).wait_recv())
+            fold(
+                rout.at[step, target, part(0)],
+                [row_in.at[step, right - 1, up] for right in range(1, width)],
+            )
+            col_final(step, up).start()
+
+        def line_of(right):
+            target = chip_at(0, right)
+            each(1, tall, lambda up: col_copy(step, up, right).wait_recv())
+            fold(
+                rout.at[step, target, part(1)],
+                [col_in.at[step, up - 1, right] for up in range(1, tall)],
+            )
+            row_final(step, right).start()
+
+        each(1, tall, column)
+        each(1, width, line_of)
+
+    def exchange_end(step):
+        each(1, width, lambda right: row_copy(step, 0, right).wait_recv())
+        each(1, tall, lambda up: col_copy(step, up, 0).wait_recv())
+        each(1, tall, lambda up: col_final(step, up).wait_recv())
+        each(1, width, lambda right: row_final(step, right).wait_recv())
+        fold(
+            rout.at[step, chip, part(0)],
+            [row_in.at[step, right - 1, 0] for right in range(1, width)]
+            + [col_end.at[step, up - 1] for up in range(1, tall)],
+        )
+        fold(
+            rout.at[step, chip, part(1)],
+            [col_in.at[step, up - 1, 0] for up in range(1, tall)]
+            + [row_end.at[step, right - 1] for right in range(1, width)],
+        )
 
     def reduce_on(step):
         for ahead in range(max(depth - 2, 0), -1, -1):
@@ -563,23 +699,33 @@
     pl.semaphore_wait(barrier, owners - 1)
     for step in range(steps):
         state = adjoint if step == 0 else hist.at[step - 1, subs]
-        re, im = state.at[:, 0], state.at[:, 1]
-        for way in range(2):
-
-            @pl.when(goes_on(way, 1))
-            def _(way=way):
-                line_copy(step, way, 1, re).start()
-
-        def plane(offset, carry, step=step, im=im):
-            near_copy(step, offset, im).start()
-            return carry
-
-        lax.fori_loop(1, chips, plane, 0)
-        for turn in range(1, pair):
-            near_mate(step, chip, turn, im).start()
-            line_mate(step, level, turn, re).start()
-        keep_im = pltpu.make_async_copy(im, near_block(step, chip, core), local.at[2])
-        keep_re = pltpu.make_async_copy(re, line_block(step, core, level), local.at[3])
+        for k in range(pieces):
+            for way in range(2):
+
+                @pl.when(goes_on(way, 1))
+                def _(way=way, k=k):
+                    line_copy(step, way, 1, k, state.at[part(k), 0]).start()
+
+        def first(right, k, step=step, state=state):
+            near_copy(step, 0, right, k, state.at[part(k), 1], chip, chip_at(0, right)).start()
+
+        def other(up, k, step=step, state=state):
+            near_copy(step, up, 0, k, state.at[part(k), 1], chip, chip_at(up, 0)).start()
+
+        each(1, width, lambda right: first(right, 0))
+        each(1, tall, lambda up: other(up, 1))
+        each(1, width, lambda right: first(right, 1))
+        each(1, tall, lambda up: other(up, 0))
+        for k in range(pieces):
+            for turn in range(1, pair):
+                near_mate(step, chip, turn, k, state.at[part(k), 1]).start()
+                line_mate(step, level, turn, k, state.at[part(k), 0]).start()
+        keep_im = pltpu.make_async_copy(
+            state.at[:, 1], near[step].at[pl.ds((chip * pair + core) * count, count)], local.at[2]
+        )
+        keep_re = pltpu.make_async_copy(
+            state.at[:, 0], line[step].at[pl.ds((core * depth + level) * count, count)], local.at[3]
+        )
         keep_im.start()
         keep_re.start()
         if step == 0:
@@ -593,24 +739,28 @@
             for sub in range(subs):
                 project(step - 1, sub)
         if depth > 1:
-            take_line(step, 1)
+            take_line(step, 1, 0)
+        take_first(step)
+        for k in range(1, pieces):
+            if depth > 1:
+                take_line(step, 1, k)
+        take_second(step)
         keep_im.wait()
         keep_re.wait()
-        take_near(step)
+        take_far(step)
+        reduce_start(step, 0, 1)
         if depth > 2:
-            take_line(step, 2)
-        reduce_start(step)
+            for k in range(pieces):
+                take_line(step, 2, k)
+        reduce_start(step, 1, depth)
         for hop in range(3, depth):
-            take_line(step, hop)
+            for k in range(pieces):
+                take_line(step, hop, k)
         mates_line(step)
         exchange(step)
         reduce_on(step)
-
-        def collect(offset, carry, step=step):
-            r_copy(step, offset).wait_recv()
-            return carry
-
-        lax.fori_loop(1, chips, collect, 0)
+        exchange_on(step)
+        exchange_end(step)
         join(step, state)
         for half in range(halves):
             rotate(step, half)
@@ -622,31 +772,49 @@
                         result.start()
 
         for hop in range(1, depth):
-            for way in range(2):
-
-                @pl.when(goes_on(way, hop))
-                def _(way=way, hop=hop):
-                    a_level = level - (hop - 1) if way == 0 else level + (hop - 1)
-                    line_copy(step, way, hop, line_block(step, core, a_level)).wait_send()
-
-        def done_chip(offset, carry, step=step):
-            near_copy(step, offset, near_block(step, chip, core)).wait_send()
-            r_copy(step, offset).wait_send()
-            return carry
-
-        lax.fori_loop(1, chips, done_chip, 0)
+            for k in range(pieces):
+                for way in range(2):
+
+                    @pl.when(goes_on(way, hop))
+                    def _(way=way, hop=hop, k=k):
+                        a_level = level - (hop - 1) if way == 0 else level + (hop - 1)
+                        block = line_block(step, core, a_level, k)
+                        line_copy(step, way, hop, k, block).wait_send()
+
+        def done_near(up, right, step=step):
+            for k in range(pieces):
+                block = near_block(step, chip, core, k)
+                near_copy(step, up, right, k, block, chip, chip).wait_send()
+
+        def done_chip(at, step=step):
+            up, right = split(at, width)
+            done_near(up, right)
+
+            @pl.when(right > 0)
+            def _():
+                row_copy(step, up, right).wait_send()
+
+            @pl.when(up > 0)
+            def _():
+                col_copy(step, up, right).wait_send()
+
+        each(1, chips, done_chip)
+        each(1, tall, lambda up: col_final(step, up).wait_send())
+        each(1, width, lambda right: row_final(step, right).wait_send())
         for turn in range(1, pair):
 
-            def done_near(a_chip, carry, step=step, turn=turn):
-                near_mate(step, a_chip, turn, near_block(step, a_chip, core)).wait_send()
-                return carry
-
-            def done_line(a_level, carry, step=step, turn=turn):
-                line_mate(step, a_level, turn, line_block(step, core, a_level)).wait_send()
-                return carry
-
-            lax.fori_loop(0, chips, done_near, 0)
-            lax.fori_loop(0, depth, done_line, 0)
+            def sent_near(a_chip, step=step, turn=turn):
+                for k in range(pieces):
+                    block = near_block(step, a_chip, core, k)
+                    near_mate(step, a_chip, turn, k, block).wait_send()
+
+            def sent_line(a_level, step=step, turn=turn):
+                for k in range(pieces):
+                    block = line_block(step, core, a_level, k)
+                    line_mate(step, a_level, turn, k, block).wait_send()
+
+            each(0, chips, sent_near)
+            each(0, depth, sent_line)
 
         def done_z(a_level, carry, step=step):
             @pl.when(a_level != level)
@@ -689,6 +857,8 @@
     others = max(chips - 1, 1)
     mates = max(pair - 1, 1)
     half = (count,) + block[2:]
+    bit = (count // pieces,) + block[2:]
+    tall = nodes // pair
     table = (depth + chips) * count * 2 * modes
     dma = pltpu.SemaphoreType.DMA
     state, grad = pl.pallas_call(
@@ -706,7 +876,10 @@
             pltpu.VMEM((steps, depth) + half, BF16),
             pltpu.VMEM((steps, 2, depth) + half, BF16),
             pltpu.VMEM((steps, chips) + half, BF16),
-            pltpu.VMEM((steps, others) + half, BF16),
+            pltpu.VMEM((steps, max(width - 1, 1), tall) + bit, BF16),
+            pltpu.VMEM((steps, max(tall - 1, 1), width) + bit, BF16),
+            pltpu.VMEM((steps, max(width - 1, 1)) + bit, BF16),
+            pltpu.VMEM((steps, max(tall - 1, 1)) + bit, BF16),
             pltpu.VMEM((batch, dim, 2 * dim), F32),
             pltpu.VMEM((steps * halves, owners, batch * rows, 2 * dim), BF16),
             pltpu.VMEM((steps * halves, owners - 1, batch * rows, 2 * dim), BF16),
@@ -714,19 +887,27 @@
             pltpu.VMEM((subs, dim, count * 2 * dim), BF16),
             pltpu.SMEM((table,), jnp.int32),
             pltpu.SMEM((table,), F32),
+            pltpu.SMEM((2, owners), jnp.int32),
+            pltpu.SMEM((2, owners), F32),
             pltpu.SMEM((depth + chips, 2, modes, count), jnp.int32),
-            dma((steps, others)),
-            dma((steps, others)),
-            dma((steps, mates, chips)),
-            dma((steps, mates, chips)),
-            dma((steps, 2, hops)),
-            dma((steps, 2, hops)),
-            dma((steps, mates, depth)),
-            dma((steps, mates, depth)),
+            dma((steps, others, pieces)),
+            dma((steps, others, pieces)),
+            dma((steps, mates, chips, pieces)),
+            dma((steps, mates, chips, pieces)),
+            dma((steps, 2, hops, pieces)),
+            dma((steps, 2, hops, pieces)),
+            dma((steps, mates, depth, pieces)),
+            dma((steps, mates, depth, pieces)),
             dma((steps, depth, pieces)),
             dma((steps, 2, depth, pieces)),
-            dma((steps, others)),
-            dma((steps, others)),
+            dma((steps, max(width - 1, 1), tall)),
+            dma((steps, max(width - 1, 1), tall)),
+            dma((steps, max(tall - 1, 1), width)),
+            dma((steps, max(tall - 1, 1), width)),
+            dma((steps, max(width - 1, 1))),
+            dma((steps, max(width - 1, 1))),
+            dma((steps, max(tall - 1, 1))),
+            dma((steps, max(tall - 1, 1))),
             dma((depth + chips,)),
             dma((depth + chips,)),
             dma((steps * halves,)),

time: 124 us -> 114 us (0.919)
  Pallas kernels: 120 us -> 110 us
    pallas_call x1, Pallas kernels: 120 us -> 110 us  [body(): pl.pallas_call(functools.partial(kernel, (nodes, depth, width, pair, coun...]
where the time goes in v2:
time: 114 us; the launch traced here: 113 us
  Pallas kernels  110 us (96%)
  local copies, waits for them, and re-layouts  3.26 us (3%)
    pallas_call x1, Pallas kernels, body(): pl.pallas_call(functools.partial(kernel, (nodes, depth, width, pair, coun...  110 us
    unnamed x2, local copies, waits for them, and re-layouts  3.26 us

profile of v2, /device:TPU:0, one launch (start us, length us, event | category | flops | bytes accessed | tf_op | source)
XLA Modules:
  0.0 113.5 jit_solution(14435004986527710615)
XLA Ops:
  0.6 109.6 %shard_map.104 = (bf16[8,2,128,128]{3,2,1,0:T(8,128)(2,1)}, f32[4,8,2,128]{3,2,1,0:T(2,128)}) custom-call(s32[4,256]{1,0:T(4,128)} %bitcast.3, s32[4,256]{1,0:T(4,128)} %bitcast.4, s32[2,4,8]{2,1,0:T(4,128)} %bitcast.5, f32[2,4]{1,0:T(2,128)} %rates.1, f32[8]{0:T(128)} %decay.1, bf16[8,2,128,128]{3,2,1,0:T(8,128)(2,1)} %adjoint.1, ...), custom_call_target="tpu_custom_call" | custom-call | tf_op jit(solution)/shard_map/pallas_call | solution.py:864
  110.2 1.9 %copy.13 = bf16[8,2,128,128]{3,2,1,0:T(8,128)(2,1)} copy(bf16[8,2,128,128]{3,2,1,0:T(8,128)(2,1)} %get-tuple-element.4) | data formatting | bytes 1048576
  112.1 1.4 %copy.14 = f32[4,8,2,128]{3,2,1,0:T(2,128)} copy(f32[4,8,2,128]{3,2,1,0:T(2,128)} %get-tuple-element.5) | data formatting | bytes 65536

commit v3 on v2

--- a/solution.py
+++ b/solution.py
@@ -415,14 +415,18 @@
                 total = total + lax.dot_general(
                     kept, both, (((0,), (0,)), ((), ())), preferred_element_type=F32
                 )
-        terms[sub % batch] = total
-        if sub % batch == batch - 1:
+        terms[step * subs + sub] = total
+        if step == steps - 1 and sub % batch == batch - 1:
             spread(step * halves + sub // batch)
 
     def spread(group):
         for target in range(owners):
             term_stage[group, target] = jnp.concatenate(
-                [terms[i, target * rows : (target + 1) * rows] for i in range(batch)], axis=0
+                [
+                    terms[group * batch + i, target * rows : (target + 1) * rows]
+                    for i in range(batch)
+                ],
+                axis=0,
             ).astype(BF16)
 
         def send(offset, carry):
@@ -511,10 +515,14 @@
             return jnp.logical_and(level >= hop - 1, level < depth - 1)
         return jnp.logical_and(level + hop - 1 < depth, level > 0)
 
-    def take_line(step, hop, k):
+    def take_line(step, hop, k, chosen=None):
         for way in range(2):
-
-            @pl.when(arrives(way, hop))
+            due = arrives(way, hop)
+            if chosen is not None:
+                onward = goes_on(way, hop + 1)
+                due = jnp.logical_and(due, onward if chosen else jnp.logical_not(onward))
+
+            @pl.when(due)
             def _(way=way):
                 a_level = level - hop if way == 0 else level + hop
                 block = line_block(step, core, a_level, k)
@@ -674,29 +682,28 @@
             + [row_end.at[step, right - 1] for right in range(1, width)],
         )
 
-    def reduce_on(step):
-        for ahead in range(max(depth - 2, 0), -1, -1):
-            for k in range(pieces):
-                for way in range(2):
-                    if way == 0:
-                        a_level = level + ahead
-                        fits = jnp.logical_and(level > 0, a_level < depth)
-                    else:
-                        a_level = level - ahead
-                        fits = jnp.logical_and(level < depth - 1, a_level >= 0)
-
-                    @pl.when(fits)
-                    def _(way=way, k=k, a_level=a_level):
-                        z_copy(step, way, a_level, k).wait_recv()
-                        for j in range(k * piece, (k + 1) * piece):
-                            total = zout[step, a_level, j].astype(F32)
-                            total = total + zin[step, way, a_level, j].astype(F32)
-                            zout[step, a_level, j] = total.astype(BF16)
-                        if ahead > 0:
-                            z_copy(step, way, a_level, k).start()
+    def reduce_on(step, ahead):
+        for k in range(pieces):
+            for way in range(2):
+                if way == 0:
+                    a_level = level + ahead
+                    fits = jnp.logical_and(level > 0, a_level < depth)
+                else:
+                    a_level = level - ahead
+                    fits = jnp.logical_and(level < depth - 1, a_level >= 0)
+
+                @pl.when(fits)
+                def _(way=way, k=k, a_level=a_level):
+                    z_copy(step, way, a_level, k).wait_recv()
+                    fold(
+                        zout.at[step, a_level, part(k)], [zin.at[step, way, a_level, part(k)]]
+                    )
+                    if ahead > 0:
+                        z_copy(step, way, a_level, k).start()
 
     prepare()
     pl.semaphore_wait(barrier, owners - 1)
+    each_ladder(lambda copy: copy.start())
     for step in range(steps):
         state = adjoint if step == 0 else hist.at[step - 1, subs]
         for k in range(pieces):
@@ -729,7 +736,6 @@
         keep_im.start()
         keep_re.start()
         if step == 0:
-            each_ladder(lambda copy: copy.start())
             fetch.wait()
             for sub in range(subs):
                 turn_saved(sub)
@@ -751,16 +757,26 @@
         reduce_start(step, 0, 1)
         if depth > 2:
             for k in range(pieces):
-                take_line(step, 2, k)
+                take_line(step, 2, k, True)
         reduce_start(step, 1, depth)
+        reduce_on(step, depth - 2)
+        if depth > 2:
+            for k in range(pieces):
+                take_line(step, 2, k, False)
         for hop in range(3, depth):
             for k in range(pieces):
                 take_line(step, hop, k)
         mates_line(step)
         exchange(step)
-        reduce_on(step)
+        for ahead in range(depth - 3, 0, -1):
+            reduce_on(step, ahead)
         exchange_on(step)
+        if depth != 2:
+            reduce_on(step, 0)
         exchange_end(step)
+        if step > 0:
+            for half in range(halves):
+                spread((step - 1) * halves + half)
         join(step, state)
         for half in range(halves):
             rotate(step, half)
@@ -880,7 +896,7 @@
             pltpu.VMEM((steps, max(tall - 1, 1), width) + bit, BF16),
             pltpu.VMEM((steps, max(width - 1, 1)) + bit, BF16),
             pltpu.VMEM((steps, max(tall - 1, 1)) + bit, BF16),
-            pltpu.VMEM((batch, dim, 2 * dim), F32),
+            pltpu.VMEM((steps * subs, dim, 2 * dim), F32),
             pltpu.VMEM((steps * halves, owners, batch * rows, 2 * dim), BF16),
             pltpu.VMEM((steps * halves, owners - 1, batch * rows, 2 * dim), BF16),
             pltpu.VMEM(saved.shape, BF16),

time: 114 us -> 97.9 us (0.86)
  Pallas kernels: 110 us -> 93.7 us
    pallas_call x1, Pallas kernels: 110 us -> 93.7 us  [body(): pl.pallas_call(functools.partial(kernel, (nodes, depth, width, pair, coun...]
where the time goes in v3:
time: 97.9 us; the launch traced here: 97.6 us
  Pallas kernels  93.7 us (96%)
  local copies, waits for them, and re-layouts  3.26 us (3%)
    pallas_call x1, Pallas kernels, body(): pl.pallas_call(functools.partial(kernel, (nodes, depth, width, pair, coun...  93.7 us
    unnamed x2, local copies, waits for them, and re-layouts  3.26 us

profile of v3, /device:TPU:0, one launch (start us, length us, event | category | flops | bytes accessed | tf_op | source)
XLA Modules:
  0.0 97.6 jit_solution(690213674048666431)
XLA Ops:
  0.6 93.7 %shard_map.104 = (bf16[8,2,128,128]{3,2,1,0:T(8,128)(2,1)}, f32[4,8,2,128]{3,2,1,0:T(2,128)}) custom-call(s32[4,256]{1,0:T(4,128)} %bitcast.3, s32[4,256]{1,0:T(4,128)} %bitcast.4, s32[2,4,8]{2,1,0:T(4,128)} %bitcast.5, f32[2,4]{1,0:T(2,128)} %rates.1, f32[8]{0:T(128)} %decay.1, bf16[8,2,128,128]{3,2,1,0:T(8,128)(2,1)} %adjoint.1, ...), custom_call_target="tpu_custom_call" | custom-call | tf_op jit(solution)/shard_map/pallas_call | solution.py:880
  94.4 1.9 %copy.13 = bf16[8,2,128,128]{3,2,1,0:T(8,128)(2,1)} copy(bf16[8,2,128,128]{3,2,1,0:T(8,128)(2,1)} %get-tuple-element.4) | data formatting | bytes 1048576
  96.2 1.4 %copy.14 = f32[4,8,2,128]{3,2,1,0:T(2,128)} copy(f32[4,8,2,128]{3,2,1,0:T(2,128)} %get-tuple-element.5) | data formatting | bytes 65536

commit v4 on v3

--- a/solution.py
+++ b/solution.py
@@ -25,7 +25,7 @@
     decay,
     adjoint,
     saved_in,
-    propagators,
+    propagators_in,
     coupling,
     out,
     grad,
@@ -71,7 +71,11 @@
     ladder_recv,
     term_send,
     term_recv,
+    hello,
+    again,
     local,
+    propagators,
+    held,
     *gathered,
 ):
     nodes, depth, width, pair, count, modes, steps, subs, dim, halves, pieces = dims
@@ -117,11 +121,39 @@
         other = lax.rem(own + offset, owners)
         return (other // cores, lax.rem(other, cores))
 
-    def greet(offset, carry):
-        pl.semaphore_signal(barrier, inc=1, device_id=owner_id(offset), device_id_type=MESH)
-        return carry
-
-    lax.fori_loop(1, owners, greet, 0)
+    def each(lo, hi, act):
+        def one(i, carry):
+            act(i)
+            return carry
+
+        lax.fori_loop(lo, hi, one, 0)
+
+    def signal(semaphore, device):
+        pl.semaphore_signal(semaphore, inc=1, device_id=device, device_id_type=MESH)
+
+    def greet_levels(semaphore):
+        def greet(other):
+            pl.when(other != level)(lambda: signal(semaphore, level_id(other)))
+
+        each(0, depth, greet)
+
+    def greet_mates(semaphore):
+        for turn in range(1, pair):
+            signal(semaphore, mate_id(turn))
+
+    def greet_chips(semaphore):
+        def greet(other):
+            pl.when(other != chip)(lambda: signal(semaphore, chip_id(other)))
+
+        each(0, chips, greet)
+
+    greet_levels(barrier)
+    greet_chips(barrier)
+    greet_mates(barrier)
+    load_u = pltpu.make_async_copy(propagators_in, propagators, local.at[4])
+    load_u.start()
+    load = pltpu.make_async_copy(adjoint, held, local.at[5])
+    load.start()
     fetch = pltpu.make_async_copy(saved_in, saved, local.at[0])
     fetch.start()
 
@@ -297,7 +329,7 @@
         lax.fori_loop(0, depth, one_level, 0)
         lax.fori_loop(0, chips, one_chip, 0)
 
-    def tabulate():
+    def note_own():
         for way in range(2):
             for mode in range(modes):
                 for j in range(count):
@@ -318,7 +350,8 @@
 
         lax.fori_loop(0, owners, locate, 0)
 
-        def entry(at, along_z):
+    def tabulate(along_z):
+        def entry(at):
             index, j = split(at, count)
             if along_z:
                 target, kind, row = node * cores + index * width + column, 0, index
@@ -334,18 +367,9 @@
                     place[slot] = home[kind, source] + member
                     weight[slot] = inside[kind, source] * value
 
-        def entry_z(at, carry):
-            entry(at, True)
-            return carry
-
-        def entry_r(at, carry):
-            entry(at, False)
-            return carry
-
-        lax.fori_loop(0, depth * count, entry_z, 0)
-        lax.fori_loop(0, chips * count, entry_r, 0)
-
-    def partial(blocks, row, put):
+        each(0, (depth if along_z else chips) * count, entry)
+
+    def partial(blocks, row, k, put):
         operator = coupling[...]
 
         def some(pick, carry):
@@ -369,7 +393,7 @@
                 put(pick * 2 + i, value.astype(BF16))
             return carry
 
-        lax.fori_loop(0, count // 2, some, 0)
+        lax.fori_loop(k * piece // 2, (k + 1) * piece // 2, some, 0)
 
     def prepare():
         def one(at, carry):
@@ -417,9 +441,10 @@
                 )
         terms[step * subs + sub] = total
         if step == steps - 1 and sub % batch == batch - 1:
+            stage(step * halves + sub // batch)
             spread(step * halves + sub // batch)
 
-    def spread(group):
+    def stage(group):
         for target in range(owners):
             term_stage[group, target] = jnp.concatenate(
                 [
@@ -429,6 +454,7 @@
                 axis=0,
             ).astype(BF16)
 
+    def spread(group):
         def send(offset, carry):
             pltpu.make_async_remote_copy(
                 src_ref=term_stage.at[group, lax.rem(own + offset, owners)],
@@ -542,13 +568,6 @@
                 for turn in range(1, pair):
                     line_mate(step, a_level, turn, k, block).start()
 
-    def each(lo, hi, act):
-        def one(i, carry):
-            act(i)
-            return carry
-
-        lax.fori_loop(lo, hi, one, 0)
-
     def take_first(step):
         def along(right):
             block, a_chip = near_got(step, 0, right, 0)
@@ -612,14 +631,17 @@
             def put(j, value):
                 zout[step, a_level, j] = value
 
-            partial(near[step], a_level, put)
-
-            def send(way):
-                for k in range(pieces):
-                    z_copy(step, way, a_level, k).start()
-
-            pl.when(jnp.logical_and(level == 0, a_level > 0))(lambda: send(0))
-            pl.when(jnp.logical_and(level == depth - 1, a_level < depth - 1))(lambda: send(1))
+            for k in range(pieces):
+                partial(near[step], a_level, k, put)
+
+                @pl.when(jnp.logical_and(level == 0, a_level > 0))
+                def _(k=k):
+                    z_copy(step, 0, a_level, k).start()
+
+                @pl.when(jnp.logical_and(level == depth - 1, a_level < depth - 1))
+                def _(k=k):
+                    z_copy(step, 1, a_level, k).start()
+
             return carry
 
         lax.fori_loop(lo, hi, one, 0)
@@ -632,11 +654,14 @@
             def put(j, value):
                 rout[step, target, j] = value
 
-            partial(line[step], depth + target, put)
+            partial(line[step], depth + target, 0, put)
 
             @pl.when(right > 0)
             def _():
                 row_copy(step, up, right).start()
+
+            for k in range(1, pieces):
+                partial(line[step], depth + target, k, put)
 
             @pl.when(up > 0)
             def _():
@@ -701,8 +726,7 @@
                     if ahead > 0:
                         z_copy(step, way, a_level, k).start()
 
-    prepare()
-    pl.semaphore_wait(barrier, owners - 1)
+    pl.semaphore_wait(barrier, depth + chips + pair - 3)
     each_ladder(lambda copy: copy.start())
     for step in range(steps):
         state = adjoint if step == 0 else hist.at[step - 1, subs]
@@ -736,17 +760,28 @@
         keep_im.start()
         keep_re.start()
         if step == 0:
+            greet_levels(hello)
+            load_u.wait()
+            prepare()
             fetch.wait()
             for sub in range(subs):
                 turn_saved(sub)
+            note_own()
             take_ladders()
-            tabulate()
+            tabulate(True)
         else:
             for sub in range(subs):
                 project(step - 1, sub)
         if depth > 1:
             take_line(step, 1, 0)
         take_first(step)
+        if step == 0:
+            tabulate(False)
+            pl.semaphore_wait(hello, depth - 1)
+            greet_mates(again)
+        else:
+            for half in range(halves):
+                stage((step - 1) * halves + half)
         for k in range(1, pieces):
             if depth > 1:
                 take_line(step, 1, k)
@@ -774,10 +809,14 @@
         if depth != 2:
             reduce_on(step, 0)
         exchange_end(step)
+        if step == 1:
+            pl.semaphore_wait(again, pair - 1)
         if step > 0:
             for half in range(halves):
                 spread((step - 1) * halves + half)
-        join(step, state)
+        if step == 0:
+            load.wait()
+        join(step, held if step == 0 else state)
         for half in range(halves):
             rotate(step, half)
             if step == steps - 1:
@@ -883,7 +922,7 @@
             jax.ShapeDtypeStruct(block, BF16),
             jax.ShapeDtypeStruct((rows, steps * subs, 2, dim), F32),
         ),
-        in_specs=[smem] * 5 + [vmem, hbm, vmem, vmem],
+        in_specs=[smem] * 5 + [hbm, hbm, hbm, vmem],
         out_specs=(hbm, vmem),
         scratch_shapes=[
             pltpu.VMEM((steps * subs, 2 * dim, 2 * dim), BF16),
@@ -928,7 +967,11 @@
             dma((depth + chips,)),
             dma((steps * halves,)),
             dma((steps * halves,)),
-            dma((4,)),
+            pltpu.SemaphoreType.REGULAR,
+            pltpu.SemaphoreType.REGULAR,
+            dma((6,)),
+            pltpu.VMEM(propagators.shape, BF16),
+            pltpu.VMEM(block, BF16),
             *[pltpu.VMEM((chips * pair * count, dim, dim), BF16)] * steps,
             *[pltpu.VMEM((depth * pair * count, dim, dim), BF16)] * steps,
         ],

time: 97.9 us -> 93.3 us (0.953)
  Pallas kernels: 93.7 us -> 89.1 us
    pallas_call x1, Pallas kernels: 93.7 us -> 89.1 us  [body(): pl.pallas_call(functools.partial(kernel, (nodes, depth, width, pair, coun...]
where the time goes in v4:
time: 93.3 us; the launch traced here: 93 us
  Pallas kernels  89.1 us (95%)
  local copies, waits for them, and re-layouts  3.26 us (3%)
    pallas_call x1, Pallas kernels, body(): pl.pallas_call(functools.partial(kernel, (nodes, depth, width, pair, coun...  89.1 us
    unnamed x2, local copies, waits for them, and re-layouts  3.26 us

profile of v4, /device:TPU:0, one launch (start us, length us, event | category | flops | bytes accessed | tf_op | source)
XLA Modules:
  0.0 93.0 jit_solution(15016355929347270982)
XLA Ops:
  0.6 89.1 %shard_map.104 = (bf16[8,2,128,128]{3,2,1,0:T(8,128)(2,1)}, f32[4,8,2,128]{3,2,1,0:T(2,128)}) custom-call(s32[4,256]{1,0:T(4,128)} %bitcast.3, s32[4,256]{1,0:T(4,128)} %bitcast.4, s32[2,4,8]{2,1,0:T(4,128)} %bitcast.5, f32[2,4]{1,0:T(2,128)} %rates.1, f32[8]{0:T(128)} %decay.1, bf16[8,2,128,128]{3,2,1,0:T(8,128)(2,1)} %adjoint.1, ...), custom_call_target="tpu_custom_call" | custom-call | tf_op jit(solution)/shard_map/pallas_call | solution.py:919
  89.7 1.9 %copy.13 = bf16[8,2,128,128]{3,2,1,0:T(8,128)(2,1)} copy(bf16[8,2,128,128]{3,2,1,0:T(8,128)(2,1)} %get-tuple-element.4) | data formatting | bytes 1048576
  91.6 1.4 %copy.14 = f32[4,8,2,128]{3,2,1,0:T(2,128)} copy(f32[4,8,2,128]{3,2,1,0:T(2,128)} %get-tuple-element.5) | data formatting | bytes 65536

commit v5 on v4

--- a/solution.py
+++ b/solution.py
@@ -18,15 +18,15 @@
 
 def kernel(
     dims,
-    higher,
-    lower,
-    ladder,
-    rates,
-    decay,
+    higher_in,
+    lower_in,
+    ladder_in,
+    rates_in,
+    decay_in,
     adjoint,
     saved_in,
     propagators_in,
-    coupling,
+    coupling_in,
     out,
     grad,
     right_u,
@@ -59,13 +59,10 @@
     line_take,
     z_send,
     z_recv,
-    row_send,
+    r_send,
     row_recv,
-    col_send,
     col_recv,
-    row_last,
     row_done,
-    col_last,
     col_done,
     ladder_send,
     ladder_recv,
@@ -76,6 +73,21 @@
     local,
     propagators,
     held,
+    coupling,
+    higher,
+    lower,
+    ladder,
+    rates,
+    decay,
+    table_sem,
+    early,
+    early_core,
+    early_row,
+    early_col,
+    early_z,
+    early_sent,
+    early_got,
+    early_z_got,
     *gathered,
 ):
     nodes, depth, width, pair, count, modes, steps, subs, dim, halves, pieces = dims
@@ -118,8 +130,7 @@
     own = node * cores + spot
 
     def owner_id(offset):
-        other = lax.rem(own + offset, owners)
-        return (other // cores, lax.rem(other, cores))
+        return split(split(own + offset, owners)[1], cores)
 
     def each(lo, hi, act):
         def one(i, carry):
@@ -150,6 +161,21 @@
     greet_levels(barrier)
     greet_chips(barrier)
     greet_mates(barrier)
+    tables = [
+        pltpu.make_async_copy(source, target, table_sem.at[at])
+        for at, (source, target) in enumerate(
+            (
+                (ladder_in, ladder),
+                (higher_in, higher),
+                (lower_in, lower),
+                (rates_in, rates),
+                (decay_in, decay),
+                (coupling_in, coupling),
+            )
+        )
+    ]
+    for copy in tables:
+        copy.start()
     load_u = pltpu.make_async_copy(propagators_in, propagators, local.at[4])
     load_u.start()
     load = pltpu.make_async_copy(adjoint, held, local.at[5])
@@ -181,7 +207,7 @@
         return remote(
             source,
             near_block(step, a_chip, core, k),
-            near_send.at[step, at, k],
+            near_send.at[step],
             near_recv.at[step, at, k],
             chip_id(target),
         )
@@ -198,8 +224,8 @@
         return remote(
             source,
             near_block(step, a_chip, core, k),
-            near_pass.at[step, turn - 1, a_chip, k],
-            near_take.at[step, turn - 1, a_chip, k],
+            near_pass.at[step],
+            near_take.at[step],
             mate_id(turn),
         )
 
@@ -208,7 +234,7 @@
         return remote(
             source,
             line_block(step, core, a_level, k),
-            line_send.at[step, way, hop - 1, k],
+            line_send.at[step],
             line_recv.at[step, way, hop - 1, k],
             level_id(level + 1 if way == 0 else level - 1),
         )
@@ -217,8 +243,8 @@
         return remote(
             source,
             line_block(step, core, a_level, k),
-            line_pass.at[step, turn - 1, a_level, k],
-            line_take.at[step, turn - 1, a_level, k],
+            line_pass.at[step],
+            line_take.at[step],
             mate_id(turn),
         )
 
@@ -226,7 +252,7 @@
         return remote(
             zout.at[step, a_level, pl.ds(k * piece, piece)],
             zin.at[step, way, a_level, pl.ds(k * piece, piece)],
-            z_send.at[step, a_level, k],
+            z_send.at[step],
             z_recv.at[step, way, a_level, k],
             level_id(level + 1 if way == 0 else level - 1),
         )
@@ -235,7 +261,7 @@
         return remote(
             rout.at[step, chip_at(up, right), part(0)],
             row_in.at[step, right - 1, up],
-            row_send.at[step, right - 1, up],
+            r_send.at[step],
             row_recv.at[step, right - 1, up],
             chip_id(chip_at(0, right)),
         )
@@ -244,7 +270,7 @@
         return remote(
             rout.at[step, chip_at(up, right), part(1)],
             col_in.at[step, up - 1, right],
-            col_send.at[step, up - 1, right],
+            r_send.at[step],
             col_recv.at[step, up - 1, right],
             chip_id(chip_at(up, 0)),
         )
@@ -253,7 +279,7 @@
         return remote(
             rout.at[step, chip_at(up, 0), part(0)],
             col_end.at[step, up - 1],
-            col_last.at[step, up - 1],
+            r_send.at[step],
             col_done.at[step, up - 1],
             chip_id(chip_at(up, 0)),
         )
@@ -262,22 +288,22 @@
         return remote(
             rout.at[step, chip_at(0, right), part(1)],
             row_end.at[step, right - 1],
-            row_last.at[step, right - 1],
+            r_send.at[step],
             row_done.at[step, right - 1],
             chip_id(chip_at(0, right)),
         )
 
     def ladder_level(other):
         return remote(
-            ladder, ladders.at[level], ladder_send.at[other], ladder_recv.at[level], level_id(other)
+            ladder, ladders.at[level], ladder_send, ladder_recv, level_id(other)
         )
 
     def ladder_chip(other):
         return remote(
             ladder,
             ladders.at[depth + chip],
-            ladder_send.at[depth + other],
-            ladder_recv.at[depth + chip],
+            ladder_send,
+            ladder_recv,
             chip_id(other),
         )
 
@@ -299,35 +325,10 @@
         lax.fori_loop(0, depth, one_level, 0)
         lax.fori_loop(0, chips, one_chip, 0)
 
-    def take_ladders():
-        def one_level(other, carry):
-            @pl.when(other != level)
-            def _():
-                remote(
-                    ladder,
-                    ladders.at[other],
-                    ladder_send.at[other],
-                    ladder_recv.at[other],
-                    level_id(other),
-                ).wait_recv()
-
-            return carry
-
-        def one_chip(other, carry):
-            @pl.when(other != chip)
-            def _():
-                remote(
-                    ladder,
-                    ladders.at[depth + other],
-                    ladder_send.at[depth + other],
-                    ladder_recv.at[depth + other],
-                    chip_id(other),
-                ).wait_recv()
-
-            return carry
-
-        lax.fori_loop(0, depth, one_level, 0)
-        lax.fori_loop(0, chips, one_chip, 0)
+    def passed_ladders(semaphore):
+        if depth + chips > 2:
+            passed = ladders.at[pl.ds(0, depth + chips - 2)]
+            pltpu.make_async_copy(passed, passed, semaphore).wait()
 
     def note_own():
         for way in range(2):
@@ -414,41 +415,39 @@
 
         lax.fori_loop(0, steps * subs, one, 0)
 
-    def turn_saved(sub):
-        for j in range(count):
-            kept = saved[steps - 1, sub, j].reshape(2 * dim, dim)
-            saved_t[sub, :, 2 * dim * j : 2 * dim * (j + 1)] = kept.T
+    def turn_saved(step, sub):
+        for j in range(0, count, 2):
+            for i in range(2):
+                for part in range(2):
+                    saved_t[step, sub, j // 2, part * dim : (part + 1) * dim, i * dim : (i + 1) * dim] = (
+                        saved[step, sub, j + i, part].T
+                    )
+
+    def beside(step, sub, j):
+        return jnp.concatenate(
+            [
+                jnp.concatenate([hist[step, sub, j + i, 0], hist[step, sub, j + i, 1]], axis=1)
+                for i in range(2)
+            ],
+            axis=0,
+        )
 
     def project(step, sub):
-        total = jnp.zeros((dim, 2 * dim), F32)
-        for j in range(count):
-            lam_re = hist[step, sub + 1, j, 0]
-            lam_im = hist[step, sub + 1, j, 1]
-            both = jnp.concatenate(
-                [
-                    jnp.concatenate([lam_re, lam_im], axis=1),
-                    jnp.concatenate([lam_im, -lam_re], axis=1),
-                ],
-                axis=0,
-            )
-            if step == steps - 1:
-                kept_t = saved_t[sub, :, 2 * dim * j : 2 * dim * (j + 1)]
-                total = total + dot(kept_t, both)
-            else:
-                kept = saved[step, sub, j].reshape(2 * dim, dim)
-                total = total + lax.dot_general(
-                    kept, both, (((0,), (0,)), ((), ())), preferred_element_type=F32
-                )
-        terms[step * subs + sub] = total
+        total = jnp.zeros((2 * dim, 2 * dim), F32)
+        for j in range(0, count, 2):
+            total = total + dot(saved_t[step, sub, j // 2], beside(step, sub + 1, j))
+        at = step * subs + sub
+        terms[at, :, :dim] = total[:dim, :dim] + total[dim:, dim:]
+        terms[at, :, dim:] = total[:dim, dim:] - total[dim:, :dim]
         if step == steps - 1 and sub % batch == batch - 1:
-            stage(step * halves + sub // batch)
-            spread(step * halves + sub // batch)
+            stage(sub // batch)
+            spread(sub // batch)
 
     def stage(group):
         for target in range(owners):
             term_stage[group, target] = jnp.concatenate(
                 [
-                    terms[group * batch + i, target * rows : (target + 1) * rows]
+                    terms[(steps - 1) * subs + group * batch + i, target * rows : (target + 1) * rows]
                     for i in range(batch)
                 ],
                 axis=0,
@@ -477,43 +476,163 @@
         for i in range(batch):
             for row in range(rows):
                 for part in range(2):
-                    grad[row, group * batch + i, part : part + 1, :] = total[
+                    grad[row, (steps - 1) * subs + group * batch + i, part : part + 1, :] = total[
                         i * rows + row : i * rows + row + 1, part * dim : (part + 1) * dim
                     ]
         pltpu.make_async_copy(everything, everything, term_send.at[group]).wait()
 
-    def rotate(step, half):
-        def one(sub, carry):
-            at = step * subs + sub
-            mult_r = right_u[at]
-            mult_l = left_u[at]
-            for j in range(0, count, 2):
-                rows = jnp.concatenate(
+    def rotate_one(step, sub):
+        at = step * subs + sub
+        mult_l = left_u[at]
+        rows = jnp.concatenate([beside(step, sub, j) for j in range(0, count, 2)], axis=0)
+        middles = dot(rows, right_u[at]).astype(BF16)
+        for j in range(0, count, 2):
+            middle = middles[j * dim : (j + 2) * dim]
+            stacked = jnp.concatenate(
+                [
+                    jnp.concatenate([middle[:dim, :dim], middle[dim:, :dim]], axis=1),
+                    jnp.concatenate([middle[:dim, dim:], middle[dim:, dim:]], axis=1),
+                ],
+                axis=0,
+            )
+            result = dot(mult_l, stacked).astype(BF16)
+            for i in range(2):
+                for part in range(2):
+                    hist[step, sub + 1, j + i, part] = result[
+                        part * dim : (part + 1) * dim, i * dim : (i + 1) * dim
+                    ]
+
+    def rotate(step):
+        each(0, subs, lambda sub: rotate_one(step, sub))
+
+    def add_to(target, sources):
+        total = target[...].astype(F32)
+        for source in sources:
+            total = total + source[...].astype(F32)
+        target[...] = total.astype(BF16)
+
+    def early_copy(step, kind, at, source, target, device):
+        return remote(
+            source, target, early_sent.at[step, kind], early_got.at[step, kind, at], device
+        )
+
+    def early_mate(step, turn):
+        return early_copy(
+            step,
+            0,
+            turn - 1,
+            early.at[step, lax.rem(core + turn, pair)],
+            early_core.at[step],
+            mate_id(turn),
+        )
+
+    def early_along(step, right):
+        a_column = lax.rem(column + right, width)
+        return early_copy(
+            step,
+            1,
+            right - 1,
+            early.at[step, core, a_column],
+            early_row.at[step, right - 1],
+            chip_id(chip_at(0, right)),
+        )
+
+    def early_across(step, up):
+        a_side = lax.rem(side + up, tall)
+        return early_copy(
+            step,
+            2,
+            up - 1,
+            early.at[step, core, column, a_side],
+            early_col.at[step, up - 1],
+            chip_id(chip_at(up, 0)),
+        )
+
+    def early_level(step, other, sender):
+        return remote(
+            early.at[step, core, column, side, other],
+            early_z.at[step, sender],
+            early_sent.at[step, 3],
+            early_z_got.at[step],
+            level_id(other),
+        )
+
+    def early_start(step):
+        for target in range(owners):
+            a_node, a_spot = target // cores, target % cores
+            early[step, a_node % pair, a_spot % width, a_node // pair, a_spot // width] = (
+                jnp.concatenate(
                     [
-                        jnp.concatenate(
-                            [hist[step, sub, j + i, 0], hist[step, sub, j + i, 1]], axis=1
-                        )
-                        for i in range(2)
+                        terms[step * subs + sub, target * rows : (target + 1) * rows]
+                        for sub in range(subs)
                     ],
                     axis=0,
-                )
-                middle = dot(rows, mult_r).astype(BF16)
-                stacked = jnp.concatenate(
-                    [
-                        jnp.concatenate([middle[:dim, :dim], middle[dim:, :dim]], axis=1),
-                        jnp.concatenate([middle[:dim, dim:], middle[dim:, dim:]], axis=1),
-                    ],
-                    axis=0,
-                )
-                result = dot(mult_l, stacked).astype(BF16)
-                for i in range(2):
-                    for part in range(2):
-                        hist[step, sub + 1, j + i, part] = result[
-                            part * dim : (part + 1) * dim, i * dim : (i + 1) * dim
-                        ]
-            return carry
-
-        lax.fori_loop(half * batch, (half + 1) * batch, one, 0)
+                ).astype(BF16)
+            )
+        for turn in range(1, pair):
+            early_mate(step, turn).start()
+
+    def early_rows(step):
+        for turn in range(1, pair):
+            early_mate(step, turn).wait_recv()
+            add_to(early.at[step, core], [early_core.at[step]])
+        for right in range(1, width):
+            early_along(step, right).start()
+
+    def early_cols(step):
+        for right in range(1, width):
+            early_along(step, right).wait_recv()
+        add_to(
+            early.at[step, core, column],
+            [early_row.at[step, right - 1] for right in range(1, width)],
+        )
+        for up in range(1, tall):
+            early_across(step, up).start()
+
+    def early_levels(step):
+        for up in range(1, tall):
+            early_across(step, up).wait_recv()
+        add_to(
+            early.at[step, core, column, side],
+            [early_col.at[step, up - 1] for up in range(1, tall)],
+        )
+
+        def send(other):
+            pl.when(other != level)(lambda: early_level(step, other, level).start())
+
+        each(0, depth, send)
+
+    def early_finish(step):
+        early_z[step, level] = early[step, core, column, side, level]
+
+        if depth > 1:
+            passed = early_z.at[step, pl.ds(0, depth - 1)]
+            pltpu.make_async_copy(passed, passed, early_z_got.at[step]).wait()
+        total = early_z[step, 0].astype(F32)
+        for other in range(1, depth):
+            total = total + early_z[step, other].astype(F32)
+        for sub in range(subs):
+            for row in range(rows):
+                at = sub * rows + row
+                for part in range(2):
+                    grad[row, step * subs + sub, part : part + 1, :] = total[
+                        at : at + 1, part * dim : (part + 1) * dim
+                    ]
+        if pair > 1:
+            pltpu.make_async_copy(
+                early_core.at[step], early_core.at[step], early_sent.at[step, 0]
+            ).wait()
+        if width > 1:
+            pltpu.make_async_copy(
+                early_row.at[step], early_row.at[step], early_sent.at[step, 1]
+            ).wait()
+        if tall > 1:
+            pltpu.make_async_copy(
+                early_col.at[step], early_col.at[step], early_sent.at[step, 2]
+            ).wait()
+        if depth > 1:
+            passed = early_z.at[step, pl.ds(0, depth - 1)]
+            pltpu.make_async_copy(passed, passed, early_sent.at[step, 3]).wait()
 
     def join(step, state):
         def one(j, carry):
@@ -555,7 +674,7 @@
                 remote(
                     block,
                     block,
-                    line_send.at[step, way, hop - 1, k],
+                    line_send.at[step],
                     line_recv.at[step, way, hop - 1, k],
                     level_id(level),
                 ).wait_recv()
@@ -607,22 +726,14 @@
         each(1, tall, one)
         for turn in range(1, pair):
 
-            def two(a_chip, turn=turn):
-                for k in range(pieces):
-                    block = near_block(step, a_chip, lax.rem(core + pair - turn, pair), k)
-                    near_mate(step, a_chip, turn, k, block).wait_recv()
-
-            each(0, chips, two)
+            passed = near[step].at[pl.ds(0, chips * count)]
+            pltpu.make_async_copy(passed, passed, near_take.at[step]).wait()
 
     def mates_line(step):
         for turn in range(1, pair):
 
-            def two(a_level, turn=turn):
-                for k in range(pieces):
-                    block = line_block(step, lax.rem(core + pair - turn, pair), a_level, k)
-                    line_mate(step, a_level, turn, k, block).wait_recv()
-
-            each(0, depth, two)
+            passed = line[step].at[pl.ds(0, depth * count)]
+            pltpu.make_async_copy(passed, passed, line_take.at[step]).wait()
 
     def reduce_start(step, lo, hi):
         def one(i, carry):
@@ -727,6 +838,7 @@
                         z_copy(step, way, a_level, k).start()
 
     pl.semaphore_wait(barrier, depth + chips + pair - 3)
+    tables[0].wait()
     each_ladder(lambda copy: copy.start())
     for step in range(steps):
         state = adjoint if step == 0 else hist.at[step - 1, subs]
@@ -763,11 +875,14 @@
             greet_levels(hello)
             load_u.wait()
             prepare()
+            for copy in tables[1:]:
+                copy.wait()
             fetch.wait()
             for sub in range(subs):
-                turn_saved(sub)
+                for a_step in range(steps):
+                    turn_saved(a_step, sub)
             note_own()
-            take_ladders()
+            passed_ladders(ladder_recv)
             tabulate(True)
         else:
             for sub in range(subs):
@@ -780,12 +895,13 @@
             pl.semaphore_wait(hello, depth - 1)
             greet_mates(again)
         else:
-            for half in range(halves):
-                stage((step - 1) * halves + half)
+            early_start(step - 1)
         for k in range(1, pieces):
             if depth > 1:
                 take_line(step, 1, k)
         take_second(step)
+        if step > 0:
+            early_rows(step - 1)
         keep_im.wait()
         keep_re.wait()
         take_far(step)
@@ -794,6 +910,8 @@
             for k in range(pieces):
                 take_line(step, 2, k, True)
         reduce_start(step, 1, depth)
+        if step > 0:
+            early_cols(step - 1)
         reduce_on(step, depth - 2)
         if depth > 2:
             for k in range(pieces):
@@ -803,88 +921,74 @@
                 take_line(step, hop, k)
         mates_line(step)
         exchange(step)
+        if step > 0:
+            early_levels(step - 1)
         for ahead in range(depth - 3, 0, -1):
             reduce_on(step, ahead)
         exchange_on(step)
         if depth != 2:
             reduce_on(step, 0)
         exchange_end(step)
-        if step == 1:
+        if step == steps - 1:
             pl.semaphore_wait(again, pair - 1)
-        if step > 0:
-            for half in range(halves):
-                spread((step - 1) * halves + half)
         if step == 0:
             load.wait()
         join(step, held if step == 0 else state)
-        for half in range(halves):
-            rotate(step, half)
-            if step == steps - 1:
+        if step < steps - 1:
+            rotate(step)
+        else:
+            for half in range(halves):
+                each(half * batch, (half + 1) * batch, lambda sub: rotate_one(step, sub))
                 for sub in range(half * batch, (half + 1) * batch):
-                    project(step, sub)
                     if sub == subs - 1:
                         result = pltpu.make_async_copy(hist.at[step, subs], out, local.at[1])
                         result.start()
-
-        for hop in range(1, depth):
-            for k in range(pieces):
-                for way in range(2):
-
-                    @pl.when(goes_on(way, hop))
-                    def _(way=way, hop=hop, k=k):
-                        a_level = level - (hop - 1) if way == 0 else level + (hop - 1)
-                        block = line_block(step, core, a_level, k)
-                        line_copy(step, way, hop, k, block).wait_send()
-
-        def done_near(up, right, step=step):
-            for k in range(pieces):
-                block = near_block(step, chip, core, k)
-                near_copy(step, up, right, k, block, chip, chip).wait_send()
-
-        def done_chip(at, step=step):
-            up, right = split(at, width)
-            done_near(up, right)
-
-            @pl.when(right > 0)
-            def _():
-                row_copy(step, up, right).wait_send()
-
-            @pl.when(up > 0)
-            def _():
-                col_copy(step, up, right).wait_send()
-
-        each(1, chips, done_chip)
-        each(1, tall, lambda up: col_final(step, up).wait_send())
-        each(1, width, lambda right: row_final(step, right).wait_send())
-        for turn in range(1, pair):
-
-            def sent_near(a_chip, step=step, turn=turn):
-                for k in range(pieces):
-                    block = near_block(step, a_chip, core, k)
-                    near_mate(step, a_chip, turn, k, block).wait_send()
-
-            def sent_line(a_level, step=step, turn=turn):
-                for k in range(pieces):
-                    block = line_block(step, core, a_level, k)
-                    line_mate(step, a_level, turn, k, block).wait_send()
-
-            each(0, chips, sent_near)
-            each(0, depth, sent_line)
-
-        def done_z(a_level, carry, step=step):
-            @pl.when(a_level != level)
-            def _():
-                for k in range(pieces):
-                    z_copy(step, 0, a_level, k).wait_send()
-
-            return carry
-
-        lax.fori_loop(0, depth, done_z, 0)
-
-    each_ladder(lambda copy: copy.wait_send())
+                    project(step, sub)
+
+    def sent(source, amount, semaphore):
+        if amount > 0:
+            passed = source.at[pl.ds(0, amount)]
+            pltpu.make_async_copy(passed, passed, semaphore).wait()
+
+    for step in range(steps):
+        sent(near[step], (chips - 1) * count, near_send.at[step])
+        sent(near[step], (pair - 1) * chips * count, near_pass.at[step])
+        sent(line[step], (pair - 1) * depth * count, line_pass.at[step])
+        crossings = (width - 1) * (tall + 1) + (tall - 1) * (width + 1)
+        sent(near[step], crossings * piece, r_send.at[step])
+        sent(zout.at[step], depth - 1, z_send.at[step])
+        for a_level in range(depth):
+            ups = a_level + 1 if a_level < depth - 1 else 0
+            downs = depth - a_level if a_level > 0 else 0
+
+            @pl.when(level == a_level)
+            def _(step=step, blocks=ups + downs):
+                sent(line[step], blocks * count, line_send.at[step])
+
+    passed_ladders(ladder_send)
     result.wait()
-    for group in range(steps * halves):
-        finish(group)
+    for step in range(steps - 1):
+        early_finish(step)
+    for half in range(halves):
+        finish(half)
+
+
+def deliver(state, grad, state_out, grad_out, state_kept, grad_kept, sems):
+    into = [
+        pltpu.make_async_copy(state, state_kept, sems.at[0]),
+        pltpu.make_async_copy(grad, grad_kept, sems.at[1]),
+    ]
+    back = [
+        pltpu.make_async_copy(state_kept, state_out, sems.at[2]),
+        pltpu.make_async_copy(grad_kept, grad_out, sems.at[3]),
+    ]
+    for copy in into:
+        copy.start()
+    for arrival, leave in zip(into, back):
+        arrival.wait()
+        leave.start()
+    for copy in back:
+        copy.wait()
 
 
 def body(adjoint, saved, propagators, coupling, higher, lower, ladder, rates, decay):
@@ -904,7 +1008,6 @@
     halves = 2 if subs % 2 == 0 else 1
     batch = subs // halves
     higher, lower, ladder = higher.T, lower.T, jnp.swapaxes(ladder, 1, 2)
-    smem = pl.BlockSpec(memory_space=pltpu.SMEM)
     vmem = pl.BlockSpec(memory_space=pltpu.VMEM)
     block = adjoint.shape
     hbm = pl.BlockSpec(memory_space=pl.ANY)
@@ -914,6 +1017,8 @@
     half = (count,) + block[2:]
     bit = (count // pieces,) + block[2:]
     tall = nodes // pair
+    before = max(steps - 1, 1)
+    slab = (subs * rows, 2 * dim)
     table = (depth + chips) * count * 2 * modes
     dma = pltpu.SemaphoreType.DMA
     state, grad = pl.pallas_call(
@@ -922,7 +1027,7 @@
             jax.ShapeDtypeStruct(block, BF16),
             jax.ShapeDtypeStruct((rows, steps * subs, 2, dim), F32),
         ),
-        in_specs=[smem] * 5 + [hbm, hbm, hbm, vmem],
+        in_specs=[hbm] * 9,
         out_specs=(hbm, vmem),
         scratch_shapes=[
             pltpu.VMEM((steps * subs, 2 * dim, 2 * dim), BF16),
@@ -936,42 +1041,54 @@
             pltpu.VMEM((steps, max(width - 1, 1)) + bit, BF16),
             pltpu.VMEM((steps, max(tall - 1, 1)) + bit, BF16),
             pltpu.VMEM((steps * subs, dim, 2 * dim), F32),
-            pltpu.VMEM((steps * halves, owners, batch * rows, 2 * dim), BF16),
-            pltpu.VMEM((steps * halves, owners - 1, batch * rows, 2 * dim), BF16),
+            pltpu.VMEM((halves, owners, batch * rows, 2 * dim), BF16),
+            pltpu.VMEM((halves, owners - 1, batch * rows, 2 * dim), BF16),
             pltpu.VMEM(saved.shape, BF16),
-            pltpu.VMEM((subs, dim, count * 2 * dim), BF16),
+            pltpu.VMEM((steps, subs, count // 2, 2 * dim, 2 * dim), BF16),
             pltpu.SMEM((table,), jnp.int32),
             pltpu.SMEM((table,), F32),
             pltpu.SMEM((2, owners), jnp.int32),
             pltpu.SMEM((2, owners), F32),
             pltpu.SMEM((depth + chips, 2, modes, count), jnp.int32),
+            dma((steps,)),
             dma((steps, others, pieces)),
-            dma((steps, others, pieces)),
-            dma((steps, mates, chips, pieces)),
-            dma((steps, mates, chips, pieces)),
+            dma((steps,)),
+            dma((steps,)),
+            dma((steps,)),
             dma((steps, 2, hops, pieces)),
-            dma((steps, 2, hops, pieces)),
-            dma((steps, mates, depth, pieces)),
-            dma((steps, mates, depth, pieces)),
-            dma((steps, depth, pieces)),
+            dma((steps,)),
+            dma((steps,)),
+            dma((steps,)),
             dma((steps, 2, depth, pieces)),
-            dma((steps, max(width - 1, 1), tall)),
+            dma((steps,)),
             dma((steps, max(width - 1, 1), tall)),
             dma((steps, max(tall - 1, 1), width)),
-            dma((steps, max(tall - 1, 1), width)),
-            dma((steps, max(width - 1, 1))),
             dma((steps, max(width - 1, 1))),
             dma((steps, max(tall - 1, 1))),
-            dma((steps, max(tall - 1, 1))),
-            dma((depth + chips,)),
-            dma((depth + chips,)),
-            dma((steps * halves,)),
-            dma((steps * halves,)),
+            dma(()),
+            dma(()),
+            dma((halves,)),
+            dma((halves,)),
             pltpu.SemaphoreType.REGULAR,
             pltpu.SemaphoreType.REGULAR,
             dma((6,)),
             pltpu.VMEM(propagators.shape, BF16),
             pltpu.VMEM(block, BF16),
+            pltpu.VMEM(coupling.shape, BF16),
+            pltpu.SMEM(higher.shape, jnp.int32),
+            pltpu.SMEM(lower.shape, jnp.int32),
+            pltpu.SMEM(ladder.shape, jnp.int32),
+            pltpu.SMEM(rates.shape, F32),
+            pltpu.SMEM(decay.shape, F32),
+            dma((6,)),
+            pltpu.VMEM((before, pair, width, tall, depth) + slab, BF16),
+            pltpu.VMEM((before, width, tall, depth) + slab, BF16),
+            pltpu.VMEM((before, max(width - 1, 1), tall, depth) + slab, BF16),
+            pltpu.VMEM((before, max(tall - 1, 1), depth) + slab, BF16),
+            pltpu.VMEM((before, depth) + slab, BF16),
+            dma((before, 4)),
+            dma((before, 3, max(width - 1, tall - 1, 1))),
+            dma((before,)),
             *[pltpu.VMEM((chips * pair * count, dim, dim), BF16)] * steps,
             *[pltpu.VMEM((depth * pair * count, dim, dim), BF16)] * steps,
         ],
@@ -979,7 +1096,20 @@
             collective_id=0, has_side_effects=True, vmem_limit_bytes=63_000_000
         ),
     )(higher, lower, ladder, rates, decay, adjoint, saved, propagators, coupling)
-    return state, grad
+    return pl.pallas_call(
+        deliver,
+        out_shape=(
+            jax.ShapeDtypeStruct(state.shape, state.dtype),
+            jax.ShapeDtypeStruct(grad.shape, grad.dtype),
+        ),
+        in_specs=[hbm, hbm],
+        out_specs=(hbm, hbm),
+        scratch_shapes=[
+            pltpu.VMEM(state.shape, state.dtype),
+            pltpu.VMEM(grad.shape, grad.dtype),
+            dma((4,)),
+        ],
+    )(state, grad)
 
 
 def solution(mesh):

time: 93.3 us -> 86.2 us (0.924)
  Pallas kernels: 89.1 us -> 85.5 us
  local copies, waits for them, and re-layouts: 3.26 us -> 0 us
    pallas_call x1, Pallas kernels: 89.1 us -> 83.6 us  [body(): pl.pallas_call(functools.partial(kernel, (nodes, depth, width, pair, coun...]
    unnamed x2 -> x0, local copies, waits for them, and re-layouts: 3.26 us -> none
    pallas_call x0 -> x1, Pallas kernels: none -> 1.87 us  [body(): pl.pallas_call(deliver, out_shape=(jax.ShapeDtypeStruct(state.shape, stat...]
where the time goes in v5:
time: 86.2 us; the launch traced here: 86.1 us
  Pallas kernels  85.5 us (99%)
    pallas_call x1, Pallas kernels, body(): pl.pallas_call(functools.partial(kernel, (nodes, depth, width, pair, coun...  83.6 us
    pallas_call x1, Pallas kernels, body(): pl.pallas_call(deliver, out_shape=(jax.ShapeDtypeStruct(state.shape, stat...  1.87 us

profile of v5, /device:TPU:0, one launch (start us, length us, event | category | flops | bytes accessed | tf_op | source)
XLA Modules:
  0.0 86.1 jit_solution(16438402856390832076)
XLA Ops:
  0.6 83.6 %shard_map.104 = (bf16[8,2,128,128]{3,2,1,0:T(8,128)(2,1)}, f32[4,8,2,128]{3,2,1,0:T(2,128)}) custom-call(s32[4,256]{1,0:T(4,128)} %bitcast.3, s32[4,256]{1,0:T(4,128)} %bitcast.4, s32[2,4,8]{2,1,0:T(4,128)} %bitcast.5, f32[2,4]{1,0:T(2,128)} %rates_in.1, f32[8]{0:T(128)} %decay_in.1, bf16[8,2,128,128]{3,2,1,0:T(8,128)(2,1)} %adjoint.1, ...), custom_call_target="tpu_custom_call" | custom-call | tf_op jit(solution)/shard_map/pallas_call | solution.py:1024
  84.2 1.9 %shard_map.105 = (bf16[8,2,128,128]{3,2,1,0:T(8,128)(2,1)}, f32[4,8,2,128]{3,2,1,0:T(2,128)}) custom-call(bf16[8,2,128,128]{3,2,1,0:T(8,128)(2,1)} %get-tuple-element.4.state, f32[4,8,2,128]{3,2,1,0:T(2,128)} %get-tuple-element.5.grad), custom_call_target="tpu_custom_call" | custom-call | tf_op jit(solution)/shard_map/pallas_call | solution.py:1099

commit v6 on v5

--- a/solution.py
+++ b/solution.py
@@ -415,33 +415,49 @@
 
         lax.fori_loop(0, steps * subs, one, 0)
 
+        def accumulate(sub):
+            for step in range(steps):
+                at = step * subs + sub
+                right_u[at] = dot(right_u[at - 1], right_u[at]).astype(BF16)
+                left_u[at] = dot(left_u[at], left_u[at - 1]).astype(BF16)
+
+        each(1, subs, accumulate)
+
     def turn_saved(step, sub):
-        for j in range(0, count, 2):
-            for i in range(2):
-                for part in range(2):
-                    saved_t[step, sub, j // 2, part * dim : (part + 1) * dim, i * dim : (i + 1) * dim] = (
-                        saved[step, sub, j + i, part].T
-                    )
-
-    def beside(step, sub, j):
+        flat = jnp.concatenate(
+            [
+                jnp.concatenate([saved[step, sub, j, part].T for part in range(2)], axis=1)
+                for j in range(count)
+            ],
+            axis=0,
+        )
+        turned = dot(flat, left_u[step * subs + sub]).astype(BF16)
+        for j in range(count):
+            for part in range(2):
+                saved_t[step, sub, part * dim : (part + 1) * dim, j * dim : (j + 1) * dim] = turned[
+                    j * dim : (j + 1) * dim, part * dim : (part + 1) * dim
+                ]
+
+    def flatten(step):
         return jnp.concatenate(
             [
-                jnp.concatenate([hist[step, sub, j + i, 0], hist[step, sub, j + i, 1]], axis=1)
-                for i in range(2)
+                jnp.concatenate([hist[step, 0, j, part] for part in range(2)], axis=1)
+                for j in range(count)
             ],
             axis=0,
         )
 
-    def project(step, sub):
-        total = jnp.zeros((2 * dim, 2 * dim), F32)
-        for j in range(0, count, 2):
-            total = total + dot(saved_t[step, sub, j // 2], beside(step, sub + 1, j))
-        at = step * subs + sub
-        terms[at, :, :dim] = total[:dim, :dim] + total[dim:, dim:]
-        terms[at, :, dim:] = total[:dim, dim:] - total[dim:, :dim]
-        if step == steps - 1 and sub % batch == batch - 1:
-            stage(sub // batch)
-            spread(sub // batch)
+    def project(step, lo, hi):
+        total = dot(
+            saved_t[step, lo:hi].reshape((hi - lo) * 2 * dim, count * dim), flatten(step)
+        )
+        for sub in range(lo, hi):
+            at = step * subs + sub
+            top = total[(sub - lo) * 2 * dim : (sub - lo) * 2 * dim + dim]
+            low = total[(sub - lo) * 2 * dim + dim : (sub - lo + 1) * 2 * dim]
+            re = top[:, :dim] + low[:, dim:]
+            im = top[:, dim:] - low[:, :dim]
+            terms[at] = dot(jnp.concatenate([re, im], axis=1).astype(BF16), right_u[at])
 
     def stage(group):
         for target in range(owners):
@@ -481,11 +497,10 @@
                     ]
         pltpu.make_async_copy(everything, everything, term_send.at[group]).wait()
 
-    def rotate_one(step, sub):
-        at = step * subs + sub
+    def rotate(step):
+        at = step * subs + subs - 1
         mult_l = left_u[at]
-        rows = jnp.concatenate([beside(step, sub, j) for j in range(0, count, 2)], axis=0)
-        middles = dot(rows, right_u[at]).astype(BF16)
+        middles = dot(flatten(step), right_u[at]).astype(BF16)
         for j in range(0, count, 2):
             middle = middles[j * dim : (j + 2) * dim]
             stacked = jnp.concatenate(
@@ -498,12 +513,9 @@
             result = dot(mult_l, stacked).astype(BF16)
             for i in range(2):
                 for part in range(2):
-                    hist[step, sub + 1, j + i, part] = result[
+                    hist[step, 1, j + i, part] = result[
                         part * dim : (part + 1) * dim, i * dim : (i + 1) * dim
                     ]
-
-    def rotate(step):
-        each(0, subs, lambda sub: rotate_one(step, sub))
 
     def add_to(target, sources):
         total = target[...].astype(F32)
@@ -841,7 +853,7 @@
     tables[0].wait()
     each_ladder(lambda copy: copy.start())
     for step in range(steps):
-        state = adjoint if step == 0 else hist.at[step - 1, subs]
+        state = adjoint if step == 0 else hist.at[step - 1, 1]
         for k in range(pieces):
             for way in range(2):
 
@@ -873,20 +885,16 @@
         keep_re.start()
         if step == 0:
             greet_levels(hello)
-            load_u.wait()
-            prepare()
             for copy in tables[1:]:
                 copy.wait()
-            fetch.wait()
-            for sub in range(subs):
-                for a_step in range(steps):
-                    turn_saved(a_step, sub)
             note_own()
             passed_ladders(ladder_recv)
             tabulate(True)
         else:
             for sub in range(subs):
-                project(step - 1, sub)
+                turn_saved(step - 1, sub)
+            for half in range(halves):
+                project(step - 1, half * batch, (half + 1) * batch)
         if depth > 1:
             take_line(step, 1, 0)
         take_first(step)
@@ -926,6 +934,13 @@
         for ahead in range(depth - 3, 0, -1):
             reduce_on(step, ahead)
         exchange_on(step)
+        if step == 0:
+            load_u.wait()
+            prepare()
+            fetch.wait()
+        if step == steps - 1:
+            for sub in range(subs):
+                turn_saved(step, sub)
         if depth != 2:
             reduce_on(step, 0)
         exchange_end(step)
@@ -934,16 +949,14 @@
         if step == 0:
             load.wait()
         join(step, held if step == 0 else state)
-        if step < steps - 1:
-            rotate(step)
-        else:
+        if step == steps - 1:
             for half in range(halves):
-                each(half * batch, (half + 1) * batch, lambda sub: rotate_one(step, sub))
-                for sub in range(half * batch, (half + 1) * batch):
-                    if sub == subs - 1:
-                        result = pltpu.make_async_copy(hist.at[step, subs], out, local.at[1])
-                        result.start()
-                    project(step, sub)
+                project(step, half * batch, (half + 1) * batch)
+                stage(half)
+                spread(half)
+        rotate(step)
+    result = pltpu.make_async_copy(hist.at[steps - 1, 1], out, local.at[1])
+    result.start()
 
     def sent(source, amount, semaphore):
         if amount > 0:
@@ -1032,7 +1045,7 @@
         scratch_shapes=[
             pltpu.VMEM((steps * subs, 2 * dim, 2 * dim), BF16),
             pltpu.VMEM((steps * subs, 2 * dim, 2 * dim), BF16),
-            pltpu.VMEM((steps, subs + 1) + block, BF16),
+            pltpu.VMEM((steps, 2) + block, BF16),
             pltpu.VMEM((steps, depth) + half, BF16),
             pltpu.VMEM((steps, 2, depth) + half, BF16),
             pltpu.VMEM((steps, chips) + half, BF16),
@@ -1044,7 +1057,7 @@
             pltpu.VMEM((halves, owners, batch * rows, 2 * dim), BF16),
             pltpu.VMEM((halves, owners - 1, batch * rows, 2 * dim), BF16),
             pltpu.VMEM(saved.shape, BF16),
-            pltpu.VMEM((steps, subs, count // 2, 2 * dim, 2 * dim), BF16),
+            pltpu.VMEM((steps, subs, 2 * dim, count * dim), BF16),
             pltpu.SMEM((table,), jnp.int32),
             pltpu.SMEM((table,), F32),
             pltpu.SMEM((2, owners), jnp.int32),

time: 86.2 us -> 83.5 us (0.969)
  Pallas kernels: 85.5 us -> 82.7 us
    pallas_call x1, Pallas kernels: 83.6 us -> 80.8 us  [body(): pl.pallas_call(functools.partial(kernel, (nodes, depth, width, pair, coun...]
where the time goes in v6:
time: 83.5 us; the launch traced here: 83.3 us
  Pallas kernels  82.7 us (99%)
    pallas_call x1, Pallas kernels, body(): pl.pallas_call(functools.partial(kernel, (nodes, depth, width, pair, coun...  80.8 us
    pallas_call x1, Pallas kernels, body(): pl.pallas_call(deliver, out_shape=(jax.ShapeDtypeStruct(state.shape, stat...  1.87 us

profile of v6, /device:TPU:0, one launch (start us, length us, event | category | flops | bytes accessed | tf_op | source)
XLA Modules:
  0.0 83.3 jit_solution(2237881371751083282)
XLA Ops:
  0.6 80.8 %shard_map.104 = (bf16[8,2,128,128]{3,2,1,0:T(8,128)(2,1)}, f32[4,8,2,128]{3,2,1,0:T(2,128)}) custom-call(s32[4,256]{1,0:T(4,128)} %bitcast.3, s32[4,256]{1,0:T(4,128)} %bitcast.4, s32[2,4,8]{2,1,0:T(4,128)} %bitcast.5, f32[2,4]{1,0:T(2,128)} %rates_in.1, f32[8]{0:T(128)} %decay_in.1, bf16[8,2,128,128]{3,2,1,0:T(8,128)(2,1)} %adjoint.1, ...), custom_call_target="tpu_custom_call" | custom-call | tf_op jit(solution)/shard_map/pallas_call | solution.py:1037
  81.5 1.9 %shard_map.105 = (bf16[8,2,128,128]{3,2,1,0:T(8,128)(2,1)}, f32[4,8,2,128]{3,2,1,0:T(2,128)}) custom-call(bf16[8,2,128,128]{3,2,1,0:T(8,128)(2,1)} %get-tuple-element.4.state, f32[4,8,2,128]{3,2,1,0:T(2,128)} %get-tuple-element.5.grad), custom_call_target="tpu_custom_call" | custom-call | tf_op jit(solution)/shard_map/pallas_call | solution.py:1112

commit v7 on v6

--- a/solution.py
+++ b/solution.py
@@ -769,7 +769,7 @@
 
         lax.fori_loop(lo, hi, one, 0)
 
-    def exchange(step):
+    def exchange(step, lo, hi):
         def one(i):
             up, right = split(chips - 1 - i, width)
             target = chip_at(up, right)
@@ -790,7 +790,7 @@
             def _():
                 col_copy(step, up, right).start()
 
-        each(0, chips, one)
+        each(lo, hi, one)
 
     def exchange_on(step):
         def column(up):
@@ -830,8 +830,8 @@
             + [row_end.at[step, right - 1] for right in range(1, width)],
         )
 
-    def reduce_on(step, ahead):
-        for k in range(pieces):
+    def reduce_on(step, ahead, some):
+        for k in some:
             for way in range(2):
                 if way == 0:
                     a_level = level + ahead
@@ -888,8 +888,6 @@
             for copy in tables[1:]:
                 copy.wait()
             note_own()
-            passed_ladders(ladder_recv)
-            tabulate(True)
         else:
             for sub in range(subs):
                 turn_saved(step - 1, sub)
@@ -899,16 +897,18 @@
             take_line(step, 1, 0)
         take_first(step)
         if step == 0:
-            tabulate(False)
-            pl.semaphore_wait(hello, depth - 1)
-            greet_mates(again)
+            passed_ladders(ladder_recv)
+            tabulate(True)
         else:
             early_start(step - 1)
         for k in range(1, pieces):
             if depth > 1:
                 take_line(step, 1, k)
         take_second(step)
-        if step > 0:
+        if step == 0:
+            pl.semaphore_wait(hello, depth - 1)
+            greet_mates(again)
+        else:
             early_rows(step - 1)
         keep_im.wait()
         keep_re.wait()
@@ -920,7 +920,10 @@
         reduce_start(step, 1, depth)
         if step > 0:
             early_cols(step - 1)
-        reduce_on(step, depth - 2)
+        reduce_on(step, depth - 2, [0])
+        if step == 0:
+            tabulate(False)
+            reduce_on(step, depth - 2, range(1, pieces))
         if depth > 2:
             for k in range(pieces):
                 take_line(step, 2, k, False)
@@ -928,11 +931,14 @@
             for k in range(pieces):
                 take_line(step, hop, k)
         mates_line(step)
-        exchange(step)
+        exchange(step, 0, chips // 2)
+        if step > 0:
+            reduce_on(step, depth - 2, range(1, pieces))
+        exchange(step, chips // 2, chips)
         if step > 0:
             early_levels(step - 1)
         for ahead in range(depth - 3, 0, -1):
-            reduce_on(step, ahead)
+            reduce_on(step, ahead, range(pieces))
         exchange_on(step)
         if step == 0:
             load_u.wait()
@@ -942,7 +948,7 @@
             for sub in range(subs):
                 turn_saved(step, sub)
         if depth != 2:
-            reduce_on(step, 0)
+            reduce_on(step, 0, range(pieces))
         exchange_end(step)
         if step == steps - 1:
             pl.semaphore_wait(again, pair - 1)

time: 83.5 us -> 82.6 us (0.989)
  Pallas kernels: 82.7 us -> 81.8 us
    pallas_call x1, Pallas kernels: 80.8 us -> 79.9 us  [body(): pl.pallas_call(functools.partial(kernel, (nodes, depth, width, pair, coun...]
where the time goes in v7:
time: 82.6 us; the launch traced here: 82.4 us
  Pallas kernels  81.8 us (99%)
    pallas_call x1, Pallas kernels, body(): pl.pallas_call(functools.partial(kernel, (nodes, depth, width, pair, coun...  79.9 us
    pallas_call x1, Pallas kernels, body(): pl.pallas_call(deliver, out_shape=(jax.ShapeDtypeStruct(state.shape, stat...  1.87 us

profile of v7, /device:TPU:0, one launch (start us, length us, event | category | flops | bytes accessed | tf_op | source)
XLA Modules:
  0.0 82.4 jit_solution(6668660210877108173)
XLA Ops:
  0.6 79.9 %shard_map.104 = (bf16[8,2,128,128]{3,2,1,0:T(8,128)(2,1)}, f32[4,8,2,128]{3,2,1,0:T(2,128)}) custom-call(s32[4,256]{1,0:T(4,128)} %bitcast.3, s32[4,256]{1,0:T(4,128)} %bitcast.4, s32[2,4,8]{2,1,0:T(4,128)} %bitcast.5, f32[2,4]{1,0:T(2,128)} %rates_in.1, f32[8]{0:T(128)} %decay_in.1, bf16[8,2,128,128]{3,2,1,0:T(8,128)(2,1)} %adjoint.1, ...), custom_call_target="tpu_custom_call" | custom-call | tf_op jit(solution)/shard_map/pallas_call | solution.py:1043
  80.5 1.9 %shard_map.105 = (bf16[8,2,128,128]{3,2,1,0:T(8,128)(2,1)}, f32[4,8,2,128]{3,2,1,0:T(2,128)}) custom-call(bf16[8,2,128,128]{3,2,1,0:T(8,128)(2,1)} %get-tuple-element.4.state, f32[4,8,2,128]{3,2,1,0:T(2,128)} %get-tuple-element.5.grad), custom_call_target="tpu_custom_call" | custom-call | tf_op jit(solution)/shard_map/pallas_call | solution.py:1118

commit v8 on v7

--- a/solution.py
+++ b/solution.py
@@ -235,7 +235,7 @@
             source,
             line_block(step, core, a_level, k),
             line_send.at[step],
-            line_recv.at[step, way, hop - 1, k],
+            line_recv.at[step, a_level, k],
             level_id(level + 1 if way == 0 else level - 1),
         )
 
@@ -253,7 +253,7 @@
             zout.at[step, a_level, pl.ds(k * piece, piece)],
             zin.at[step, way, a_level, pl.ds(k * piece, piece)],
             z_send.at[step],
-            z_recv.at[step, way, a_level, k],
+            z_recv.at[step, a_level + (1 - way), k],
             level_id(level + 1 if way == 0 else level - 1),
         )
 
@@ -472,7 +472,7 @@
     def spread(group):
         def send(offset, carry):
             pltpu.make_async_remote_copy(
-                src_ref=term_stage.at[group, lax.rem(own + offset, owners)],
+                src_ref=term_stage.at[group, split(own + offset, owners)[1]],
                 dst_ref=term_inbox.at[group, offset - 1],
                 send_sem=term_send.at[group],
                 recv_sem=term_recv.at[group],
@@ -687,7 +687,7 @@
                     block,
                     block,
                     line_send.at[step],
-                    line_recv.at[step, way, hop - 1, k],
+                    line_recv.at[step, a_level, k],
                     level_id(level),
                 ).wait_recv()
                 if hop + 1 < depth:
@@ -993,14 +993,14 @@
 
 
 def deliver(state, grad, state_out, grad_out, state_kept, grad_kept, sems):
-    into = [
-        pltpu.make_async_copy(state, state_kept, sems.at[0]),
-        pltpu.make_async_copy(grad, grad_kept, sems.at[1]),
-    ]
-    back = [
-        pltpu.make_async_copy(state_kept, state_out, sems.at[2]),
-        pltpu.make_async_copy(grad_kept, grad_out, sems.at[3]),
-    ]
+    pieces = state.shape[0]
+    into = [pltpu.make_async_copy(grad, grad_kept, sems.at[0])]
+    back = [pltpu.make_async_copy(grad_kept, grad_out, sems.at[1])]
+    for at in range(pieces):
+        into.append(pltpu.make_async_copy(state.at[at], state_kept.at[at], sems.at[2 + 2 * at]))
+        back.append(
+            pltpu.make_async_copy(state_kept.at[at], state_out.at[at], sems.at[3 + 2 * at])
+        )
     for copy in into:
         copy.start()
     for arrival, leave in zip(into, back):
@@ -1074,11 +1074,11 @@
             dma((steps,)),
             dma((steps,)),
             dma((steps,)),
-            dma((steps, 2, hops, pieces)),
+            dma((steps, depth, pieces)),
             dma((steps,)),
             dma((steps,)),
             dma((steps,)),
-            dma((steps, 2, depth, pieces)),
+            dma((steps, depth + 1, pieces)),
             dma((steps,)),
             dma((steps, max(width - 1, 1), tall)),
             dma((steps, max(tall - 1, 1), width)),
@@ -1126,7 +1126,7 @@
         scratch_shapes=[
             pltpu.VMEM(state.shape, state.dtype),
             pltpu.VMEM(grad.shape, grad.dtype),
-            dma((4,)),
+            dma((2 + 2 * state.shape[0],)),
         ],
     )(state, grad)
 

time: 82.6 us -> 82.4 us (level)
  no operation moved by 1% of the time
where the time goes in v8:
time: 82.4 us; the launch traced here: 82.2 us
  Pallas kernels  81.6 us (99%)
    pallas_call x1, Pallas kernels, body(): pl.pallas_call(functools.partial(kernel, (nodes, depth, width, pair, coun...  79.7 us
    pallas_call x1, Pallas kernels, body(): pl.pallas_call(deliver, out_shape=(jax.ShapeDtypeStruct(state.shape, stat...  1.87 us

profile of v8, /device:TPU:0, one launch (start us, length us, event | category | flops | bytes accessed | tf_op | source)
XLA Modules:
  0.0 82.2 jit_solution(16288020311839789683)
XLA Ops:
  0.6 79.7 %shard_map.104 = (bf16[8,2,128,128]{3,2,1,0:T(8,128)(2,1)}, f32[4,8,2,128]{3,2,1,0:T(2,128)}) custom-call(s32[4,256]{1,0:T(4,128)} %bitcast.3, s32[4,256]{1,0:T(4,128)} %bitcast.4, s32[2,4,8]{2,1,0:T(4,128)} %bitcast.5, f32[2,4]{1,0:T(2,128)} %rates_in.1, f32[8]{0:T(128)} %decay_in.1, bf16[8,2,128,128]{3,2,1,0:T(8,128)(2,1)} %adjoint.1, ...), custom_call_target="tpu_custom_call" | custom-call | tf_op jit(solution)/shard_map/pallas_call | solution.py:1043
  80.4 1.9 %shard_map.105 = (bf16[8,2,128,128]{3,2,1,0:T(8,128)(2,1)}, f32[4,8,2,128]{3,2,1,0:T(2,128)}) custom-call(bf16[8,2,128,128]{3,2,1,0:T(8,128)(2,1)} %get-tuple-element.4.state, f32[4,8,2,128]{3,2,1,0:T(2,128)} %get-tuple-element.5.grad), custom_call_target="tpu_custom_call" | custom-call | tf_op jit(solution)/shard_map/pallas_call | solution.py:1118
